TPU v7x, 512 devices: a whole 4x4x16 slice. The times are simulated.
512 devices in a mesh: grp: 64 (over y_lo, z, core), tp: 8 (over x, y_hi).
Axes of the slice: x: 4, y: 4 (y_hi: 2, y_lo: 2; y = y_hi * 2 + y_lo), z: 16, core: 2. Of those that a mesh axis runs over, the one named last changes fastest.
Arguments:
- queries: bfloat16 [64, 2, 512, 2048], P('grp', None, None, 'tp'), may hold values from -9 to 9
- fresh_kv: bfloat16 [64, 2, 512, 2, 2048], P('grp', None, None, None, 'tp'), may hold values from -9 to 9
- stale_kv: bfloat16 [64, 2, 512, 2, 2048], P('grp', None, None, None, 'tp'), may hold values from -6 to 6
- text_kv: bfloat16 [64, 2, 256, 2, 2048], P('grp', None, None, None, 'tp'), may hold values from -6 to 6
- w_velocity: bfloat16 [2048, 64], P('tp'), may hold values from -2.390625 to 2.390625
- latent: float32 [64, 2, 512, 64], P('grp', None, 'tp'), may hold values from -6 to 6
- live_counts: int32 [64, 2], replicated, may hold values from 128 to 512, as said below
- refresh_rows: int32 [64, 2, 64], replicated, may hold values from 0 to 511, as said below
- request_list: int32 [64], replicated, may hold values from 0 to 63, each once
- timesteps: int32 [64, 2], replicated, may hold values from 0 to 999, as said below
Outputs:
- next_stale: bfloat16 [64, 2, 512, 2, 2048], P('grp', None, None, None, 'tp')
- velocity: float32 [64, 2, 512, 64], P('grp', None, 'tp')
- latent_next: float32 [64, 2, 512, 64], P('grp', None, 'tp')
Inputs may be any that keep to these rules, and one draw needn't show every extreme that they name: `live_counts`: 512 is reached in every draw. `refresh_rows`: rows within one list are distinct. `timesteps`: the next timestep is below the current one. `request_list`: each request appears once.
All inputs are finite; a program needn't handle non-finite values.
Results may differ from a plain program's by a relative error of at most 0.0045.
Values may be sent and summed in bfloat16 or wider, within the bound.
A program may use at most 64 MiB of HBM per device.

v0:
```python
import math

import jax
import jax.numpy as jnp
from jax import lax
from jax.sharding import PartitionSpec as P

HD = 128


def from_behind(block, axis, distance):
    devices = range(lax.axis_size(axis))
    route = [((i - distance) % len(devices), i) for i in devices]
    return lax.ppermute(block, axis, route)


def slot_velocity(slot_query, own_kv, partner_kv, text_pair, own_live, partner_live, w_velocity):
    img_rows = slot_query.shape[0]
    heads_here = slot_query.shape[1] // HD
    key_rows = jnp.concatenate([own_kv[:, 0], partner_kv[:, 0], text_pair[:, 0]], axis=0)
    value_rows = jnp.concatenate([own_kv[:, 1], partner_kv[:, 1], text_pair[:, 1]], axis=0)
    row_ids = jnp.arange(img_rows, dtype=jnp.int32)
    live_mask = jnp.concatenate(
        [row_ids < own_live, row_ids < partner_live, jnp.ones((text_pair.shape[0],), dtype=bool)]
    )
    outputs = []
    for head_index in range(heads_here):
        first = head_index * HD
        scores = lax.dot_general(
            slot_query[:, first : first + HD],
            key_rows[:, first : first + HD],
            (((1,), (1,)), ((), ())),
            preferred_element_type=jnp.float32,
        ) * (1.0 / math.sqrt(HD))
        scores = jnp.where(live_mask[None, :], scores, -jnp.inf)
        row_top = jnp.max(scores, axis=1, keepdims=True)
        weights = jnp.exp(scores - row_top)
        totals = jnp.sum(weights, axis=1, keepdims=True)
        blended = (
            jnp.dot(
                weights.astype(jnp.bfloat16),
                value_rows[:, first : first + HD],
                preferred_element_type=jnp.float32,
            )
            / totals
        )
        outputs.append(blended.astype(jnp.bfloat16))
    blended = jnp.concatenate(outputs, axis=1)
    return jnp.dot(blended, w_velocity, preferred_element_type=jnp.float32)


def shards(
    queries,
    fresh_kv,
    stale_kv,
    text_kv,
    w_velocity,
    latent,
    live_counts,
    refresh_rows,
    request_list,
    timesteps,
):
    groups_count = lax.axis_size("grp")
    half_groups = groups_count // 2
    my_group = lax.axis_index("grp")
    partner = (my_group + half_groups) % groups_count
    slot_count = queries.shape[1]
    partner_fresh = from_behind(fresh_kv, "grp", half_groups)
    text_other = from_behind(text_kv, "grp", half_groups)
    partner_lists = lax.dynamic_index_in_dim(refresh_rows, partner, 0, keepdims=False)
    my_live = lax.dynamic_index_in_dim(live_counts, my_group, 0, keepdims=False)
    partner_live = lax.dynamic_index_in_dim(live_counts, partner, 0, keepdims=False)
    arrived = jnp.stack(
        [
            jnp.take(partner_fresh[0, slot_index], partner_lists[slot_index], axis=0)
            for slot_index in range(slot_count)
        ]
    )
    partials = []
    for slot_index in range(slot_count):
        repaired = stale_kv[0, slot_index].at[partner_lists[slot_index]].set(arrived[slot_index])
        text_pair = jnp.concatenate([text_kv[0, slot_index], text_other[0, slot_index]], axis=0)
        partials.append(
            slot_velocity(
                queries[0, slot_index],
                fresh_kv[0, slot_index],
                repaired,
                text_pair,
                my_live[slot_index],
                partner_live[slot_index],
                w_velocity,
            )
        )
    partial_value = jnp.stack(partials)
    tp_count = lax.axis_size("tp")
    share = partial_value.shape[1] // tp_count
    tp_index = lax.axis_index("tp")
    whole = lax.psum(partial_value, "tp")
    summed = lax.dynamic_slice_in_dim(whole, tp_index * share, share, 1)
    row_ids = tp_index * share + jnp.arange(share, dtype=jnp.int32)
    live_rows = row_ids[None, :] < my_live[:, None]
    velocity = jnp.where(live_rows[:, :, None], summed, 0.0)
    pair_index = my_group % half_groups
    request_ids = lax.dynamic_slice_in_dim(request_list, pair_index * slot_count, slot_count)
    matches = (
        request_ids[:, None] == jnp.arange(timesteps.shape[0], dtype=jnp.int32)[None, :]
    ).astype(jnp.int32)
    times = jnp.dot(matches, timesteps)
    step_size = (times[:, 1] - times[:, 0]).astype(jnp.float32) / 1000.0
    latent_next = latent[0] + step_size[:, None, None] * velocity
    return (partner_fresh, velocity[None], latent_next[None])


def solution(mesh):
    return jax.shard_map(
        shards,
        mesh=mesh,
        in_specs=(
            P("grp", None, None, "tp"),
            P("grp", None, None, None, "tp"),
            P("grp", None, None, None, "tp"),
            P("grp", None, None, None, "tp"),
            P("tp", None),
            P("grp", None, "tp", None),
            P(),
            P(),
            P(),
            P(),
        ),
        out_specs=(
            P("grp", None, None, None, "tp"),
            P("grp", None, "tp", None),
            P("grp", None, "tp", None),
        ),
        check_vma=False,
    )
```

profile of v0, /device:TPU:6, one launch (start us, length us, event | category | flops | bytes accessed | tf_op | source)
XLA Modules:
  0.0 190.6 jit_solution(1452022395850017873)
XLA Ops:
  7.3 1.2 copy.61
  8.5 3.5 %collective-permute-start.1 = (bf16[1,2,256,2,256]{4,2,3,1,0:T(8,128)(2,1)S(1)}, bf16[1,2,256,2,256]{4,2,3,1,0:T(8,128)(2,1)}, u32[]{:S(2)}, u32[]{:S(2)}) collective-permute-start(bf16[1,2,256,2,256]{4,2,3,1,0:T(8,128)(2,1)S(1)} %copy.61), channel_id=1, source_target_pairs={{256,0},{264,8},{272,16},{280,24},{288,32},{296,40},{304,48},{312,... | collective-permute-start | bytes 1572872 | tf_op jit(solution)/shard_map/ppermute | solution.py:14
  12.0 2.4 %collective-permute-start = (bf16[1,2,512,2,256]{4,3,2,1,0:T(2,128)(2,1)}, bf16[1,2,512,2,256]{4,3,2,1,0:T(2,128)(2,1)S(1)}, u32[]{:S(2)}, u32[]{:S(2)}) collective-permute-start(bf16[1,2,512,2,256]{4,3,2,1,0:T(2,128)(2,1)} %param.13), channel_id=1, source_target_pairs={{256,0},{264,8},{272,16},{280,24},{288,32},{296,40},{304,48},{312,... | collective-permute-start | bytes 3145736 | tf_op jit(solution)/shard_map/ppermute | solution.py:14
  15.4 0.8 slice_bitcast_fusion.10
  16.3 1.9 %fusion.83 = (bf16[1,1,512,2,256]{4,3,2,1,0:T(2,128)(2,1)S(1)}, bf16[1,1,512,2,256]{4,3,2,1,0:T(2,128)(2,1)S(1)}) fusion(bf16[1,2,512,2,256]{4,3,2,1,0:T(2,128)(2,1)} %param.13), kind=kLoop, calls=%fused_computation.132 | loop fusion | bytes 2097152 | tf_op jit(solution)/shard_map/slice | solution.py:87
  18.5 0.8 multiply_reduce_fusion
  23.4 0.9 slice_bitcast_fusion.4
  25.7 2.7 %slice_bitcast_fusion.3 = (bf16[512,2,256]{2,1,0:T(2,128)(2,1)S(1)}, bf16[512,2,256]{2,1,0:T(2,128)(2,1)}) fusion(bf16[1,2,512,2,256]{4,3,2,1,0:T(2,128)(2,1)} %param.14), kind=kLoop, calls=%fused_computation.55 | loop fusion | bytes 2097152 | tf_op jit(solution)/shard_map/squeeze | solution.py:82
  28.4 1.1 slice_bitcast_fusion.9
  29.5 0.9 fusion.60
  30.4 16.1 %collective-permute-done = bf16[1,2,512,2,256]{4,3,2,1,0:T(2,128)(2,1)S(1)} collective-permute-done((bf16[1,2,512,2,256]{4,3,2,1,0:T(2,128)(2,1)}, bf16[1,2,512,2,256]{4,3,2,1,0:T(2,128)(2,1)S(1)}, u32[]{:S(2)}, u32[]{:S(2)}) %collective-permute-start) | collective-permute-done | bytes 1048608 | tf_op jit(solution)/shard_map/ppermute | solution.py:14
  46.5 1.5 slice_bitcast_fusion.1
  48.0 1.8 gather_fusion
  50.5 0.9 broadcast_select_fusion
  51.4 2.6 %scatter_fusion = bf16[512,2,256]{2,1,0:T(2,128)(2,1)S(1)} fusion(bf16[512,2,256]{2,1,0:T(2,128)(2,1)S(1)} %get-tuple-element.32, s32[64]{0:T(128)S(1)} %get-tuple-element.56, bf16[64,2,256]{2,1,0:T(2,128)(2,1)S(1)} %get-tuple-element.78), kind=kCustom, calls=%fused_computation.2 | custom fusion | bytes 196864 | tf_op jit(solution)/shard_map/scatter | solution.py:82
  54.0 1.5 fusion.84
  55.7 2.2 %fusion.90 = (f32[512]{0:T(512)S(1)}, f32[1536,512]{1,0:T(8,128)}) fusion(bf16[512,256]{1,0:T(8,128)(2,1)S(1)} %copy-done.5, bf16[1536,256]{1,0:T(8,128)(2,1)S(1)} %pad_maximum_fusion, pred[1536]{0:T(1024)(128)(4,1)S(1)} %get-tuple-element.63), kind=kOutput, calls=%fused_computation.139 | convolution fusion | flops 203685376 | bytes 3674112 | tf_op jit(solution)/shard_map/dot_general | solution.py:29
  58.5 7.5 %scatter_fusion.1 = bf16[512,2,256]{2,1,0:T(2,128)(2,1)} fusion(bf16[512,2,256]{2,1,0:T(2,128)(2,1)} %get-tuple-element.33, s32[64]{0:T(128)} %get-tuple-element.57, bf16[64,2,256]{2,1,0:T(2,128)(2,1)S(1)} %get-tuple-element.77), kind=kCustom, calls=%fused_computation.3 | custom fusion | bytes 196864 | tf_op jit(solution)/shard_map/scatter | solution.py:82
  66.0 2.1 %fusion.85 = (bf16[512,1,256]{2,1,0:T(2,128)(2,1)S(1)}, bf16[512,1,256]{2,1,0:T(2,128)(2,1)S(1)}) fusion(bf16[512,2,256]{2,1,0:T(2,128)(2,1)} %scatter_fusion.1), kind=kLoop, calls=%fused_computation.134 | loop fusion | bytes 1048576 | tf_op jit(solution)/shard_map/slice | solution.py:21
  68.1 1.1 pad_maximum_fusion.2
  70.9 1.0 copy-done.1
  77.8 102.6 %all-reduce.2.cloned.1.call-done = f32[2,512,64]{1,2,0:T(8,128)} async-done(((f32[2,512,64]{1,2,0:T(8,128)}), f32[2,512,64]{1,2,0:T(8,128)}) %all-reduce.2.cloned.1.call-update) | async-done | bytes 262160 | tf_op jit(solution)/shard_map/psum | solution.py:99
  180.4 0.9 fusion.72
  182.8 1.0 copy.88
  (89 shorter events, 17.2 us)
Async XLA Ops:
  7.2 7.2 %copy-start = (s32[64,2,64]{2,1,0:T(2,128)S(1)}, s32[64,2,64]{2,1,0:T(2,128)}, u32[]{:S(2)}) copy-start(s32[64,2,64]{2,1,0:T(2,128)} %param.19) | copy-start | bytes 98308
  7.2 11.0 %copy-start.20 = (s32[64]{0:T(128)S(1)}, s32[64]{0:T(128)}, u32[]{:S(2)}) copy-start(s32[64]{0:T(128)} %param.20) | copy-start | bytes 772
  7.2 11.1 %copy-start.19 = (s32[64,2]{0,1:T(2,128)S(1)}, s32[64,2]{0,1:T(2,128)}, u32[]{:S(2)}) copy-start(s32[64,2]{0,1:T(2,128)} %param.21) | copy-start | bytes 1540
  7.2 12.0 %copy-start.15 = (s32[64,2]{0,1:T(2,128)S(1)}, s32[64,2]{0,1:T(2,128)}, u32[]{:S(2)}) copy-start(s32[64,2]{0,1:T(2,128)} %param.18) | copy-start | bytes 1540
  7.2 15.2 %copy-start.13 = (bf16[1,2,512,256]{3,2,1,0:T(8,128)(2,1)S(1)}, bf16[1,2,512,256]{3,2,1,0:T(8,128)(2,1)}, u32[]{:S(2)}) copy-start(bf16[1,2,512,256]{3,2,1,0:T(8,128)(2,1)} %param.12) | copy-start | bytes 1572868
  7.2 173.2 %all-reduce.2.cloned.1.call-start = ((), (), s32[]{:S(2)}) async-start(), calls=%async_computation | async-start | bytes 524288 | tf_op jit(solution)/shard_map/psum | solution.py:99
  8.5 20.0 %collective-permute-start.1 = (bf16[1,2,256,2,256]{4,2,3,1,0:T(8,128)(2,1)S(1)}, bf16[1,2,256,2,256]{4,2,3,1,0:T(8,128)(2,1)}, u32[]{:S(2)}, u32[]{:S(2)}) collective-permute-start(bf16[1,2,256,2,256]{4,2,3,1,0:T(8,128)(2,1)S(1)} %copy.61), channel_id=1, source_target_pairs={{256,0},{264,8},{272,16},{280,24},{288,32},{296,40},{304,48},{312,... | collective-permute-start | bytes 1572872 | tf_op jit(solution)/shard_map/ppermute | solution.py:14
  12.0 34.5 %collective-permute-start = (bf16[1,2,512,2,256]{4,3,2,1,0:T(2,128)(2,1)}, bf16[1,2,512,2,256]{4,3,2,1,0:T(2,128)(2,1)S(1)}, u32[]{:S(2)}, u32[]{:S(2)}) collective-permute-start(bf16[1,2,512,2,256]{4,3,2,1,0:T(2,128)(2,1)} %param.13), channel_id=1, source_target_pairs={{256,0},{264,8},{272,16},{280,24},{288,32},{296,40},{304,48},{312,... | collective-permute-start | bytes 3145736 | tf_op jit(solution)/shard_map/ppermute | solution.py:14
  23.3 6.2 %copy-start.10 = (bf16[256,2,256]{2,0,1:T(8,128)(2,1)S(1)}, bf16[256,2,256]{2,0,1:T(8,128)(2,1)}, u32[]{:S(2)}) copy-start(bf16[256,2,256]{2,0,1:T(8,128)(2,1)} %get-tuple-element.44) | copy-start | bytes 786436
  23.4 6.2 %copy-start.11 = (bf16[256,2,256]{2,0,1:T(8,128)(2,1)S(1)}, bf16[256,2,256]{2,0,1:T(8,128)(2,1)}, u32[]{:S(2)}) copy-start(bf16[256,2,256]{2,0,1:T(8,128)(2,1)} %get-tuple-element.45) | copy-start | bytes 786436
  30.4 25.2 %copy-start.5 = (bf16[512,256]{1,0:T(8,128)(2,1)S(1)}, bf16[512,256]{1,0:T(8,128)(2,1)}, u32[]{:S(2)}) copy-start(bf16[512,256]{1,0:T(8,128)(2,1)} %get-tuple-element.40) | copy-start | bytes 786436
  46.5 9.2 %copy-start.2 = (bf16[1,2,512,2,256]{4,3,2,1,0:T(2,128)(2,1)}, bf16[1,2,512,2,256]{4,3,2,1,0:T(2,128)(2,1)S(1)}, u32[]{:S(2)}) copy-start(bf16[1,2,512,2,256]{4,3,2,1,0:T(2,128)(2,1)S(1)} %collective-permute-done) | copy-start | bytes 3145732
  55.5 2.3 %copy-start.6 = (bf16[512,256]{1,0:T(8,128)(2,1)S(1)}, bf16[512,256]{1,0:T(8,128)(2,1)}, u32[]{:S(2)}) copy-start(bf16[512,256]{1,0:T(8,128)(2,1)} %get-tuple-element.40) | copy-start | bytes 786436
  69.8 1.0 copy-start.4
  69.8 2.1 %copy-start.1 = (f32[1536,512]{1,0:T(8,128)S(1)}, f32[1536,512]{1,0:T(8,128)}, u32[]{:S(2)}) copy-start(f32[1536,512]{1,0:T(8,128)} %get-tuple-element.70) | copy-start | bytes 9437188
  70.4 1.9 %copy-start.8 = (bf16[512,256]{1,0:T(8,128)(2,1)S(1)}, bf16[512,256]{1,0:T(8,128)(2,1)}, u32[]{:S(2)}) copy-start(bf16[512,256]{1,0:T(8,128)(2,1)} %get-tuple-element.34) | copy-start | bytes 786436
  70.4 1.9 %copy-start.12 = (bf16[512,256]{1,0:T(8,128)(2,1)S(1)}, bf16[512,256]{1,0:T(8,128)(2,1)}, u32[]{:S(2)}) copy-start(bf16[512,256]{1,0:T(8,128)(2,1)} %get-tuple-element.76) | copy-start | bytes 786436
  73.5 1.1 copy-start.7
  73.5 1.1 copy-start.9
  75.3 1.2 copy-start.18
  75.9 1.8 copy-start.14
  75.9 1.9 copy-start.17
  75.9 104.6 %copy-start.16 = (f32[2]{0:T(128)S(1)}, f32[2]{0:T(128)}, u32[]{:S(2)}) copy-start(f32[2]{0:T(128)} %multiply_reduce_fusion) | copy-start | bytes 28
  75.9 106.9 %copy-start.3 = (bf16[1,2,512,2,256]{4,3,2,1,0:T(2,128)(2,1)S(1)}, bf16[1,2,512,2,256]{4,3,2,1,0:T(2,128)(2,1)}, u32[]{:S(2)}) copy-start(bf16[1,2,512,2,256]{4,3,2,1,0:T(2,128)(2,1)} %copy-done.2) | copy-start | bytes 3145732
Sparse Core Ops, SparseCore 0:
  77.7 102.6 all-reduce.1
where the time goes:
time: 192 us; the launch traced here: 191 us
  waiting for transfers between devices  119 us (62%)
  local copies, waits for them, and re-layouts  33.5 us (17%)
  between operations  14.6 us (8%)
  other arithmetic  11.1 us (6%)
  matrix products  6.91 us (4%)
  starting transfers between devices  5.88 us (3%)
    psum x1, waiting for transfers between devices, shards(): whole = lax.psum(partial_value, 'tp')  103 us
    ppermute x2, waiting for transfers between devices, from_behind(): return lax.ppermute(block, axis, route)  16.1 us
    scatter x2, local copies, waits for them, and re-layouts, shards(): stale_kv[0, slot_index].at[partner_lists[slot_index]]  10.1 us
    ppermute x2, starting transfers between devices, from_behind(): return lax.ppermute(block, axis, route)  5.85 us
    unnamed x51, local copies, waits for them, and re-layouts  5.25 us
    dot_general x4, matrix products, slot_velocity(): lax.dot_general(slot_query[:, first:first + HD], key_rows[:, first:first...  3.98 us
  transfers between devices with their start and end apart: 3, of which 2 were waited for; matrix products, arithmetic and copies ran while one was open for 8% of the time, Pallas kernels for 0%

commit v1 on v0

v1 whole, which is shorter than its diff:
```python
import math

import jax
import jax.numpy as jnp
from jax import lax
from jax.experimental.layout import Layout, with_layout_constraint
from jax.experimental import pallas as pl
from jax.experimental.pallas import tpu as pltpu
from jax.sharding import PartitionSpec as P

HD = 128
TILE = 128
SCALE = math.log2(math.e) / math.sqrt(HD)
VMEM = pltpu.MemorySpace.VMEM
SMEM = pltpu.MemorySpace.SMEM


def whole(space):
    return pl.BlockSpec(memory_space=space)


def from_behind(block, axis, distance):
    devices = range(lax.axis_size(axis))
    route = [((i - distance) % len(devices), i) for i in devices]
    return lax.ppermute(block, axis, route)


def swap_rows(lists, group, sub, flag, free, rows, listed):
    keep = rows - listed
    slots = sub.shape[0]
    step = 8

    def over(body, first):
        return lax.fori_loop(0, listed // step, body, first)

    def ids(i):
        return [(s, i * step + k) for k in range(step) for s in range(slots)]

    def clear(i, carry):
        for s, j in ids(i):
            flag[s, j] = 0
        return carry

    over(clear, 0)

    def mark(i, carry):
        found = [(s, lists[group, s, j]) for s, j in ids(i)]
        for s, row in found:
            flag[s, jnp.where(row >= keep, row - keep, listed)] = 1
        return carry

    over(mark, 0)

    def collect(i, counts):
        counts = list(counts)
        taken = [(s, j, flag[s, j]) for s, j in ids(i)]
        for s, j, used in taken:
            free[s, counts[s]] = j + keep
            counts[s] = counts[s] + (1 - used)
        return tuple(counts)

    over(collect, (0,) * slots)

    def assign(i, counts):
        counts = list(counts)
        found = [(s, j, lists[group, s, j]) for s, j in ids(i)]
        result = []
        for s, j, row in found:
            low = row < keep
            result.append((s, j, jnp.where(low, free[s, counts[s]], row)))
            counts[s] = counts[s] + low.astype(jnp.int32)
        for s, j, row in result:
            sub[s, j] = row
        return tuple(counts)

    over(assign, (0,) * slots)


def pack_kernel(lists, fresh, early, bulk, held, sub, flag, free, in_sem, out_sem):
    _, slots, rows, _, _ = fresh.shape
    listed = early.shape[2]
    keep = rows - listed
    group = lax.axis_index("grp")
    loads = [
        pltpu.make_async_copy(fresh.at[0, s], held.at[s], in_sem.at[s])
        for s in range(slots)
    ]
    for load in loads:
        load.start()
    stores = []
    swap_rows(lists, group, sub, flag, free, rows, listed)
    step = 8
    for s in range(slots):
        loads[s].wait()

        def exchange(i, carry, s=s):
            ids = [i * step + k for k in range(step)]
            at = [lists[group, s, j] for j in ids]
            to = [sub[s, j] for j in ids]
            taken = [held[s, row] for row in at]
            given = [held[s, row] for row in to]
            for k in range(step):
                early[0, s, ids[k]] = taken[k]
            for k in range(step):
                held[s, at[k]] = given[k]
            return carry

        lax.fori_loop(0, listed // step, exchange, 0)
        store = pltpu.make_async_copy(
            held.at[s, pl.ds(0, keep)], bulk.at[0, s], out_sem.at[s]
        )
        store.start()
        stores.append(store)
    for store in stores:
        store.wait()


def pack(refresh_rows, fresh_kv):
    _, slots, rows, two, width = fresh_kv.shape
    listed = refresh_rows.shape[2]
    keep = rows - listed
    kv = fresh_kv.dtype
    return pl.pallas_call(
        pack_kernel,
        out_shape=(
            jax.ShapeDtypeStruct((1, slots, listed, two, width), kv),
            jax.ShapeDtypeStruct((1, slots, keep, two, width), kv),
        ),
        in_specs=[whole(SMEM), whole(pl.ANY)],
        out_specs=(whole(VMEM), whole(pl.ANY)),
        scratch_shapes=[
            pltpu.VMEM((slots, rows, two, width), kv),
            pltpu.SMEM((slots, listed), jnp.int32),
            pltpu.SMEM((slots, listed + 1), jnp.int32),
            pltpu.SMEM((slots, listed + 1), jnp.int32),
            pltpu.SemaphoreType.DMA((slots,)),
            pltpu.SemaphoreType.DMA((slots,)),
        ],
        compiler_params=pltpu.CompilerParams(vmem_limit_bytes=8 << 20),
        cost_estimate=pl.CostEstimate(
            flops=0, transcendentals=0, bytes_accessed=4 << 20
        ),
        name="pack",
    )(refresh_rows, fresh_kv)


def place_rows(lists, group, sub, early, held, slot):
    step = 8

    def place(i, carry):
        ids = [i * step + k for k in range(step)]
        at = [lists[group, slot, j] for j in ids]
        to = [sub[slot, j] for j in ids]
        moved = [held[slot, row] for row in at]
        new = [early[0, slot, j] for j in ids]
        for k in range(step):
            held[slot, to[k]] = moved[k]
        for k in range(step):
            held[slot, at[k]] = new[k]
        return carry

    lax.fori_loop(0, early.shape[2] // step, place, 0)


def unpack_kernel(lists, sub, early, bulk, after, out, held, in_sem, out_sem):
    _, slots, rows, _, _ = out.shape
    keep = rows - early.shape[2]
    partner = lax.rem(
        lax.axis_index("grp") + lax.axis_size("grp") // 2, lax.axis_size("grp")
    )
    loads = [
        pltpu.make_async_copy(
            bulk.at[0, s], held.at[s, pl.ds(0, keep)], in_sem.at[s]
        )
        for s in range(slots)
    ]
    for load in loads:
        load.start()
    stores = []
    for s in range(slots):
        loads[s].wait()
        place_rows(lists, partner, sub, early, held, s)
        store = pltpu.make_async_copy(held.at[s], out.at[0, s], out_sem.at[s])
        store.start()
        stores.append(store)
    for store in stores:
        store.wait()


def unpack(refresh_rows, sub, early, bulk, after):
    _, slots, listed, two, width = early.shape
    rows = bulk.shape[2] + listed
    kv = bulk.dtype
    return pl.pallas_call(
        unpack_kernel,
        out_shape=jax.ShapeDtypeStruct((1, slots, rows, two, width), kv),
        in_specs=[
            whole(SMEM),
            whole(SMEM),
            whole(VMEM),
            whole(pl.ANY),
            whole(pl.ANY),
        ],
        out_specs=whole(pl.ANY),
        scratch_shapes=[
            pltpu.VMEM((slots, rows, two, width), kv),
            pltpu.SemaphoreType.DMA((slots,)),
            pltpu.SemaphoreType.DMA((slots,)),
        ],
        compiler_params=pltpu.CompilerParams(vmem_limit_bytes=8 << 20),
        cost_estimate=pl.CostEstimate(
            flops=0, transcendentals=0, bytes_accessed=4 << 20
        ),
        name="unpack",
    )(refresh_rows, sub, early, bulk, after)


def prepare_kernel(lists, live, bias, sub, flag, free):
    slots = bias.shape[0]
    listed = lists.shape[2]
    rows = (bias.shape[2] - TILE) // 2
    groups = lax.axis_size("grp")
    group = lax.axis_index("grp")
    partner = lax.rem(group + groups // 2, groups)
    ids = lax.broadcasted_iota(jnp.int32, (1, rows), 1)
    early_ids = lax.broadcasted_iota(jnp.int32, (1, TILE), 1)
    dead = jnp.float32(-jnp.inf)
    for s in range(slots):
        partner_live = live[s, partner]

        def mark(j, carry, s=s):
            stale_bias, early_row = carry
            row = lists[partner, s, j]
            stale_bias = jnp.where(ids == row, dead, stale_bias)
            early_row = jnp.where(early_ids == j, row, early_row)
            return stale_bias, early_row

        stale_bias, early_row = lax.fori_loop(
            0,
            listed,
            mark,
            (
                jnp.where(ids < partner_live, 0.0, dead),
                jnp.full((1, TILE), rows, jnp.int32),
            ),
            unroll=8,
        )
        bias[s, :, :rows] = jnp.where(ids < live[s, group], 0.0, dead)
        bias[s, :, rows : 2 * rows] = stale_bias
        bias[s, :, 2 * rows :] = jnp.where(early_row < partner_live, 0.0, dead)
    swap_rows(lists, partner, sub, flag, free, rows, listed)


def prepare(refresh_rows, live_t, rows):
    _, slots, listed = refresh_rows.shape
    return pl.pallas_call(
        prepare_kernel,
        out_shape=(
            jax.ShapeDtypeStruct((slots, 1, 2 * rows + TILE), jnp.float32),
            jax.ShapeDtypeStruct((slots, listed), jnp.int32),
        ),
        in_specs=[whole(SMEM), whole(SMEM)],
        out_specs=(whole(VMEM), whole(SMEM)),
        scratch_shapes=[
            pltpu.SMEM((slots, listed + 1), jnp.int32),
            pltpu.SMEM((slots, listed + 1), jnp.int32),
        ],
        compiler_params=pltpu.CompilerParams(vmem_limit_bytes=4 << 20),
        cost_estimate=pl.CostEstimate(
            flops=0, transcendentals=0, bytes_accessed=1 << 20
        ),
        name="prepare",
    )(refresh_rows, live_t)


def tiles(array):
    return [array[:, i : i + TILE] for i in range(0, array.shape[1], TILE)]


def attend_kernel(
    bias, q, own, stale, text, text_other, early, w_t, out, scores, acc
):
    slot, head = pl.program_id(0), pl.program_id(1)
    rows = own.shape[2]
    query = q[0, 0]
    blocks = (
        (own, bias[0, :, :rows]),
        (stale, bias[0, :, rows : 2 * rows]),
        (early, bias[0, :, 2 * rows :]),
        (text, None),
        (text_other, None),
    )
    top = None
    first = 0
    spans = []
    for block, block_bias in blocks:
        s = lax.dot_general(
            query,
            block[0, 0],
            (((1,), (1,)), ((), ())),
            preferred_element_type=jnp.float32,
        )
        if block_bias is not None:
            s = s + block_bias
        count = s.shape[1]
        scores[:, first : first + count] = s
        spans.append((first, count))
        first += count
        for tile in tiles(s):
            top = tile if top is None else jnp.maximum(top, tile)
    shift = jnp.max(top, axis=1, keepdims=True) * SCALE
    totals = None
    blended = None
    for (block, _), (first, count) in zip(blocks, spans):
        weights = jnp.exp2(scores[:, first : first + count] * SCALE - shift)
        for tile in tiles(weights):
            totals = tile if totals is None else totals + tile
        part = jnp.dot(
            weights.astype(jnp.bfloat16),
            block[0, 1],
            preferred_element_type=jnp.float32,
        )
        blended = part if blended is None else blended + part
    totals = jnp.sum(totals, axis=1, keepdims=True)
    blended = (blended / totals).astype(jnp.bfloat16)
    v = lax.dot_general(
        blended,
        w_t[...],
        (((1,), (1,)), ((), ())),
        preferred_element_type=jnp.float32,
    )

    @pl.when(head == 0)
    def _():
        acc[...] = v

    @pl.when(head > 0)
    def _():
        acc[...] += v

    width = v.shape[1]
    last = head == pl.num_programs(1) - 1

    for s in range(2):

        @pl.when(jnp.logical_and(last, slot == s))
        def _(s=s):
            out[:, s * width : (s + 1) * width] = acc[...]


def attend(bias, queries, own, stale, text, text_other, early, w_t):
    _, slots, rows, inner = queries.shape
    heads = inner // HD
    ch = w_t.shape[0]
    keys = sum(a.shape[2] for a in (own, stale, text, text_other, early))

    def kv_spec(a):
        return pl.BlockSpec((1, 2, a.shape[2], HD), lambda s, h: (s, 0, 0, h))

    return pl.pallas_call(
        attend_kernel,
        grid=(slots, heads),
        out_shape=jax.ShapeDtypeStruct((rows, slots * ch), jnp.float32),
        in_specs=[
            pl.BlockSpec((1, 1, bias.shape[2]), lambda s, h: (s, 0, 0)),
            pl.BlockSpec((1, 1, rows, HD), lambda s, h: (0, s, 0, h)),
            kv_spec(own),
            kv_spec(stale),
            kv_spec(text),
            kv_spec(text_other),
            kv_spec(early),
            pl.BlockSpec((ch, HD), lambda s, h: (0, h)),
        ],
        out_specs=pl.BlockSpec((rows, slots * ch), lambda s, h: (0, 0)),
        scratch_shapes=[
            pltpu.VMEM((rows, keys), jnp.float32),
            pltpu.VMEM((rows, ch), jnp.float32),
        ],
        compiler_params=pltpu.CompilerParams(vmem_limit_bytes=24 << 20),
        cost_estimate=pl.CostEstimate(
            flops=20 * slots * heads * rows * keys * HD,
            transcendentals=slots * heads * rows * keys,
            bytes_accessed=4 << 20,
        ),
        name="attend",
    )(bias, queries, own, stale, text, text_other, early, w_t)


def tp_sum_kernel(
    part, out, leaving, arrived, mine, crossing, other, send, recv, send2, recv2
):
    t = lax.axis_index("tp")
    x, half = t // 2, lax.rem(t, 2)
    sides = lax.axis_size("tp") // 2
    share = out.shape[0]
    pair = 2 * share
    peers = [lax.rem(x + d, sides) for d in range(1, sides)]
    across = x * 2 + 1 - half

    barrier = pltpu.get_barrier_semaphore()
    for peer in peers:
        pl.semaphore_signal(
            barrier,
            inc=1,
            device_id={"tp": peer * 2 + half},
            device_id_type=pl.DeviceIdType.MESH,
        )
    pl.semaphore_signal(
        barrier,
        inc=1,
        device_id={"tp": across},
        device_id_type=pl.DeviceIdType.MESH,
    )
    leaving[...] = part[...].astype(leaving.dtype)
    pl.semaphore_wait(barrier, sides)

    copies = []
    for i, peer in enumerate(peers):
        copy = pltpu.make_async_remote_copy(
            src_ref=leaving.at[pl.ds(pl.multiple_of(peer * pair, 16), pair)],
            dst_ref=arrived.at[i],
            send_sem=send.at[i],
            recv_sem=recv.at[i],
            device_id={"tp": peer * 2 + half},
            device_id_type=pl.DeviceIdType.MESH,
        )
        copy.start()
        copies.append(copy)
    total = part[pl.ds(pl.multiple_of(x * pair, 8), pair)]
    for i, copy in enumerate(copies):
        copy.wait_recv()
        total = total + arrived[i].astype(jnp.float32)
    mine[...] = total
    there = pl.multiple_of((1 - half) * share, 8)
    crossing[...] = mine[pl.ds(there, share)].astype(crossing.dtype)
    copy = pltpu.make_async_remote_copy(
        src_ref=crossing,
        dst_ref=other,
        send_sem=send2,
        recv_sem=recv2,
        device_id={"tp": across},
        device_id_type=pl.DeviceIdType.MESH,
    )
    copy.start()
    copy.wait_recv()
    here = pl.multiple_of(half * share, 8)
    out[...] = mine[pl.ds(here, share)] + other[...].astype(jnp.float32)
    for done in copies:
        done.wait_send()
    copy.wait_send()


def tp_sum(part, members):
    rows, width = part.shape
    share = rows // members
    sides = members // 2
    return pl.pallas_call(
        tp_sum_kernel,
        out_shape=jax.ShapeDtypeStruct((share, width), jnp.float32),
        in_specs=[whole(VMEM)],
        out_specs=whole(VMEM),
        scratch_shapes=[
            pltpu.VMEM((rows, width), jnp.bfloat16),
            pltpu.VMEM((sides - 1, 2 * share, width), jnp.bfloat16),
            pltpu.VMEM((2 * share, width), jnp.float32),
            pltpu.VMEM((share, width), jnp.bfloat16),
            pltpu.VMEM((share, width), jnp.bfloat16),
            pltpu.SemaphoreType.DMA((sides - 1,)),
            pltpu.SemaphoreType.DMA((sides - 1,)),
            pltpu.SemaphoreType.DMA,
            pltpu.SemaphoreType.DMA,
        ],
        compiler_params=pltpu.CompilerParams(
            collective_id=0, has_side_effects=True, vmem_limit_bytes=4 << 20
        ),
        cost_estimate=pl.CostEstimate(
            flops=0, transcendentals=0, bytes_accessed=4 << 20
        ),
        name="tp_sum",
    )(part)


def finish_kernel(live, requests, times, total, latent, velocity, latent_next):
    _, slots, share, ch = latent.shape
    groups = lax.axis_size("grp")
    group = lax.axis_index("grp")
    first = lax.axis_index("tp") * share
    pair = lax.rem(group, groups // 2)
    ids = first + lax.broadcasted_iota(jnp.int32, (share, ch), 0)
    for s in range(slots):
        request = requests[pair * slots + s]
        gap = times[1, request] - times[0, request]
        step = jnp.full((share, ch), gap, jnp.int32).astype(jnp.float32) / 1000.0
        v = jnp.where(ids < live[s, group], total[:, s * ch : (s + 1) * ch], 0.0)
        velocity[0, s] = v
        latent_next[0, s] = latent[0, s] + step * v


def finish(live_t, request_list, times_t, total, latent):
    return pl.pallas_call(
        finish_kernel,
        out_shape=(
            jax.ShapeDtypeStruct(latent.shape, jnp.float32),
            jax.ShapeDtypeStruct(latent.shape, jnp.float32),
        ),
        in_specs=[whole(SMEM)] * 3 + [whole(VMEM)] * 2,
        out_specs=(whole(VMEM), whole(VMEM)),
        compiler_params=pltpu.CompilerParams(vmem_limit_bytes=4 << 20),
        cost_estimate=pl.CostEstimate(
            flops=0, transcendentals=0, bytes_accessed=1 << 20
        ),
        name="finish",
    )(live_t, request_list, times_t, total, latent)


def in_order(array):
    return with_layout_constraint(array, Layout(tuple(range(array.ndim))))


def apart(kv):
    return jnp.transpose(kv[0], (0, 2, 1, 3))


def shards(
    queries,
    fresh_kv,
    stale_kv,
    text_kv,
    w_velocity,
    latent,
    live_counts,
    refresh_rows,
    request_list,
    timesteps,
):
    half_groups = lax.axis_size("grp") // 2
    live_t = live_counts.T
    times_t = timesteps.T
    rows = fresh_kv.shape[2]
    listed = refresh_rows.shape[2]
    text_other = in_order(from_behind(in_order(text_kv), "grp", half_groups))
    early_out, bulk_out = pack(refresh_rows, fresh_kv)
    early = from_behind(early_out, "grp", half_groups)
    bias, sub = prepare(refresh_rows, live_t, rows)
    text_other, bulk_out, bias, sub = lax.optimization_barrier(
        (text_other, bulk_out, bias, sub)
    )
    bulk = from_behind(bulk_out, "grp", half_groups)
    early_apart = jnp.pad(apart(early), ((0, 0), (0, 0), (0, TILE - listed), (0, 0)))
    part = attend(
        bias,
        queries,
        apart(fresh_kv),
        apart(stale_kv),
        apart(text_kv),
        apart(text_other),
        early_apart,
        w_velocity.T,
    )
    total = tp_sum(part, lax.axis_size("tp"))
    velocity, latent_next = finish(live_t, request_list, times_t, total, latent)
    next_stale = unpack(refresh_rows, sub, early, bulk, velocity)
    return next_stale, velocity, latent_next


def solution(mesh):
    return jax.shard_map(
        shards,
        mesh=mesh,
        in_specs=(
            P("grp", None, None, "tp"),
            P("grp", None, None, None, "tp"),
            P("grp", None, None, None, "tp"),
            P("grp", None, None, None, "tp"),
            P("tp", None),
            P("grp", None, "tp", None),
            P(),
            P(),
            P(),
            P(),
        ),
        out_specs=(
            P("grp", None, None, None, "tp"),
            P("grp", None, "tp", None),
            P("grp", None, "tp", None),
        ),
        check_vma=False,
    )
```

time: 192 us -> 52.3 us (0.27)
  the two profiles are of different devices: /device:TPU:6 before, /device:TPU:24 now
where the time goes in v1:
time: 52.3 us; the launch traced here: 51.9 us
  Pallas kernels  38 us (73%)
  starting transfers between devices  8.63 us (17%)
  local copies, waits for them, and re-layouts  4.35 us (8%)
  between operations  0.88 us (2%)
    pallas_call x1, Pallas kernels, tp_sum(): pl.pallas_call(tp_sum_kernel, out_shape=jax.ShapeDtypeStruct((share, widt...  14.8 us
    ppermute x3, starting transfers between devices, from_behind(): return lax.ppermute(block, axis, route)  8.63 us
    pallas_call x1, Pallas kernels, attend(): pl.pallas_call(attend_kernel, grid=(slots, heads), out_shape=jax.ShapeDty...  8.55 us
    pallas_call x1, Pallas kernels, pack(): pl.pallas_call(pack_kernel, out_shape=(jax.ShapeDtypeStruct((1, slots, li...  5.1 us
    pallas_call x1, Pallas kernels, prepare(): pl.pallas_call(prepare_kernel, out_shape=(jax.ShapeDtypeStruct((slots, 1,...  4.57 us
    unnamed x30, local copies, waits for them, and re-layouts  4.26 us
    pallas_call x1, Pallas kernels, unpack(): pl.pallas_call(unpack_kernel, out_shape=jax.ShapeDtypeStruct((1, slots, r...  3.75 us
    pallas_call x1, Pallas kernels, finish(): pl.pallas_call(finish_kernel, out_shape=(jax.ShapeDtypeStruct(latent.shap...  1.32 us
  transfers between devices with their start and end apart: 3, of which 0 were waited for; matrix products, arithmetic and copies ran while one was open for 1% of the time, Pallas kernels for 66%

profile of v1, /device:TPU:24, one launch (start us, length us, event | category | flops | bytes accessed | tf_op | source)
XLA Modules:
  0.0 51.9 jit_solution(10205862917768337474)
XLA Ops:
  0.6 2.7 %collective-permute-start = (bf16[1,2,256,2,256]{4,3,2,1,0:T(2,128)(2,1)}, bf16[1,2,256,2,256]{4,3,2,1,0:T(2,128)(2,1)S(1)}, u32[]{:S(2)}, u32[]{:S(2)}) collective-permute-start(bf16[1,2,256,2,256]{4,3,2,1,0:T(2,128)(2,1)} %param.13), channel_id=1, source_target_pairs={{256,0},{264,8},{272,16},{280,24},{288,32},{296,40},{304,48},{312,... | collective-permute-start | bytes 1572872 | tf_op jit(solution)/shard_map/ppermute | solution.py:25
  3.3 1.2 %copy-done = bf16[1,2,512,2,256]{4,3,2,1,0:T(2,128)(2,1)S(1)} copy-done((bf16[1,2,512,2,256]{4,3,2,1,0:T(2,128)(2,1)S(1)}, bf16[1,2,512,2,256]{4,3,2,1,0:T(2,128)(2,1)}, u32[]{:S(2)}) %copy-start) | copy-done | bytes 1048600
  4.5 0.8 %copy-done.2 = s32[64,2,64]{2,1,0:T(2,128)S(1)} copy-done((s32[64,2,64]{2,1,0:T(2,128)S(1)}, s32[64,2,64]{2,1,0:T(2,128)}, u32[]{:S(2)}) %copy-start.2) | copy-done | bytes 32792
  5.4 5.1 %pack.1 = (bf16[1,2,64,2,256]{4,3,2,1,0:T(2,128)(2,1)S(1)}, bf16[1,2,448,2,256]{4,3,2,1,0:T(2,128)(2,1)S(1)}) custom-call(s32[64,2,64]{2,1,0:T(2,128)S(1)} %copy-done.2, bf16[1,2,512,2,256]{4,3,2,1,0:T(2,128)(2,1)S(1)} %copy-done), custom_call_target="tpu_custom_call" | custom-call | bytes 4194304 | tf_op jit(solution)/shard_map/pack/pallas_call | solution.py:123
  10.5 0.0 copy-start.6
  10.5 3.2 %collective-permute-start.1 = (bf16[1,2,64,2,256]{4,3,2,1,0:T(2,128)(2,1)S(1)}, bf16[1,2,64,2,256]{4,3,2,1,0:T(2,128)(2,1)S(1)}, u32[]{:S(2)}, u32[]{:S(2)}) collective-permute-start(bf16[1,2,64,2,256]{4,3,2,1,0:T(2,128)(2,1)S(1)} %get-tuple-element.17), channel_id=1, source_target_pairs={{256,0},{264,8},{272,16},{280,24},{288,32},{296,40},{304,48},{312,... | collective-permute-start | bytes 393224 | tf_op jit(solution)/shard_map/ppermute | solution.py:25
  13.7 4.6 %prepare.1 = (f32[2,1,1152]{2,1,0:T(1,128)S(1)}, s32[2,64]{1,0:T(2,128)S(1)}) custom-call(s32[64,2,64]{2,1,0:T(2,128)S(1)} %copy-done.2, s32[2,64]{1,0:T(2,128)S(1)} %bitcast.31), custom_call_target="tpu_custom_call" | custom-call | bytes 1048576 | tf_op jit(solution)/shard_map/prepare/pallas_call | solution.py:256
  18.3 0.0 copy-start.12
  18.3 0.0 copy-start.11
  18.3 2.8 %collective-permute-start.2 = (bf16[1,2,448,2,256]{4,3,2,1,0:T(2,128)(2,1)S(1)}, bf16[1,2,448,2,256]{4,3,2,1,0:T(2,128)(2,1)S(1)}, u32[]{:S(2)}, u32[]{:S(2)}) collective-permute-start(bf16[1,2,448,2,256]{4,3,2,1,0:T(2,128)(2,1)S(1)} %get-tuple-element.18), channel_id=1, source_target_pairs={{256,0},{264,8},{272,16},{280,24},{288,32},{296,40},{304,48},{312,... | collective-permute-start | bytes 2752520 | tf_op jit(solution)/shard_map/ppermute | solution.py:25
  21.1 0.1 copy.24
  21.3 0.1 copy.26
  21.4 0.1 copy.23
  21.6 0.0 copy-start.10
  21.6 0.1 copy.25
  21.7 0.9 %copy-done.9 = bf16[1,2,512,256]{3,2,1,0:T(8,128)(2,1)S(1)} copy-done((bf16[1,2,512,256]{3,2,1,0:T(8,128)(2,1)S(1)}, bf16[1,2,512,256]{3,2,1,0:T(8,128)(2,1)}, u32[]{:S(2)}) %copy-start.9) | copy-done | bytes 524312
  22.6 8.5 %attend.1.part = f32[512,128]{1,0:T(8,128)S(1)} custom-call(f32[2,1,1152]{2,1,0:T(1,128)S(1)} %get-tuple-element.19.bias, bf16[1,2,512,256]{3,2,1,0:T(8,128)(2,1)S(1)} %copy-done.9, bf16[2,2,512,256]{3,2,1,0:T(8,128)(2,1)S(1)} %bitcast.26, bf16[2,2,512,256]{3,2,1,0:T(8,128)(2,1)S(1)} %bitcast.27, bf16[2,2,256,256]{3,2,1,0:T(8,128)(2,1)S(1)} %bitcast.29, ...), custom_call_target="tpu_custom_call" | custom-call | flops 8724152320 | bytes 4194304 | tf_op jit(solution)/shard_map/attend/pallas_call | solution.py:360
  31.2 0.0 copy-start.5
  31.2 14.8 %tp_sum.1.total = f32[64,128]{1,0:T(8,128)S(1)} custom-call(f32[512,128]{1,0:T(8,128)S(1)} %attend.1.part), custom_call_target="tpu_custom_call" | custom-call | bytes 4194304 | tf_op jit(solution)/shard_map/tp_sum/pallas_call | solution.py:457
  45.9 0.0 copy-start.3
  46.0 1.3 %finish.1 = (f32[1,2,64,64]{3,2,1,0:T(8,128)}, f32[1,2,64,64]{3,2,1,0:T(8,128)}) custom-call(s32[2,64]{1,0:T(2,128)S(1)} %bitcast.32, s32[64]{0:T(128)S(1)} %copy-done.8, s32[2,64]{1,0:T(2,128)S(1)} %bitcast.33, f32[64,128]{1,0:T(8,128)S(1)} %tp_sum.1.total, f32[1,2,64,64]{3,2,1,0:T(8,128)S(1)} %copy-done.5), custom_call_target="tpu_custom_call" | custom-call | bytes 1048576 | tf_op jit(solution)/shard_map/finish/pallas_call | solution.py:500
  47.3 0.0 copy-start.4
  47.3 0.8 %copy-done.4 = f32[1,2,64,64]{3,2,1,0:T(8,128)S(1)} copy-done((f32[1,2,64,64]{3,2,1,0:T(8,128)S(1)}, f32[1,2,64,64]{3,2,1,0:T(8,128)}, u32[]{:S(2)}) %copy-start.4) | copy-done | bytes 32792
  48.2 3.7 %unpack.1 = bf16[1,2,512,2,256]{4,3,2,1,0:T(2,128)(2,1)} custom-call(s32[64,2,64]{2,1,0:T(2,128)S(1)} %copy-done.3, s32[2,64]{1,0:T(2,128)S(1)} %get-tuple-element.16.sub, bf16[1,2,64,2,256]{4,3,2,1,0:T(2,128)(2,1)S(1)} %collective-permute-done.1.early, bf16[1,2,448,2,256]{4,3,2,1,0:T(2,128)(2,1)S(1)} %collective-permute-done.2.bulk, ...), custom_call_target="tpu_custom_call" | custom-call | bytes 4194304 | tf_op jit(solution)/shard_map/unpack/pallas_call | solution.py:194
  (20 shorter events, 0.1 us)
Async XLA Ops:
  0.6 17.6 %collective-permute-start = (bf16[1,2,256,2,256]{4,3,2,1,0:T(2,128)(2,1)}, bf16[1,2,256,2,256]{4,3,2,1,0:T(2,128)(2,1)S(1)}, u32[]{:S(2)}, u32[]{:S(2)}) collective-permute-start(bf16[1,2,256,2,256]{4,3,2,1,0:T(2,128)(2,1)} %param.13), channel_id=1, source_target_pairs={{256,0},{264,8},{272,16},{280,24},{288,32},{296,40},{304,48},{312,... | collective-permute-start | bytes 1572872 | tf_op jit(solution)/shard_map/ppermute | solution.py:25
  3.3 1.2 %copy-start = (bf16[1,2,512,2,256]{4,3,2,1,0:T(2,128)(2,1)S(1)}, bf16[1,2,512,2,256]{4,3,2,1,0:T(2,128)(2,1)}, u32[]{:S(2)}) copy-start(bf16[1,2,512,2,256]{4,3,2,1,0:T(2,128)(2,1)} %fresh.1) | copy-start | bytes 3145732
  4.5 0.8 %copy-start.2 = (s32[64,2,64]{2,1,0:T(2,128)S(1)}, s32[64,2,64]{2,1,0:T(2,128)}, u32[]{:S(2)}) copy-start(s32[64,2,64]{2,1,0:T(2,128)} %lists.5) | copy-start | bytes 98308
  5.4 15.7 %copy-start.1 = (bf16[1,2,512,2,256]{4,3,2,1,0:T(2,128)(2,1)S(1)}, bf16[1,2,512,2,256]{4,3,2,1,0:T(2,128)(2,1)}, u32[]{:S(2)}) copy-start(bf16[1,2,512,2,256]{4,3,2,1,0:T(2,128)(2,1)} %fresh.1) | copy-start | bytes 3145732
  10.5 3.2 %copy-start.6 = (s32[64,2]{0,1:T(2,128)S(1)}, s32[64,2]{0,1:T(2,128)}, u32[]{:S(2)}) copy-start(s32[64,2]{0,1:T(2,128)} %param.16) | copy-start | bytes 1540
  10.5 11.0 %collective-permute-start.1 = (bf16[1,2,64,2,256]{4,3,2,1,0:T(2,128)(2,1)S(1)}, bf16[1,2,64,2,256]{4,3,2,1,0:T(2,128)(2,1)S(1)}, u32[]{:S(2)}, u32[]{:S(2)}) collective-permute-start(bf16[1,2,64,2,256]{4,3,2,1,0:T(2,128)(2,1)S(1)} %get-tuple-element.17), channel_id=1, source_target_pairs={{256,0},{264,8},{272,16},{280,24},{288,32},{296,40},{304,48},{312,... | collective-permute-start | bytes 393224 | tf_op jit(solution)/shard_map/ppermute | solution.py:25
  18.3 3.0 %copy-start.12 = (bf16[1,2,256,2,256]{4,3,2,1,0:T(2,128)(2,1)S(1)}, bf16[1,2,256,2,256]{4,3,2,1,0:T(2,128)(2,1)}, u32[]{:S(2)}) copy-start(bf16[1,2,256,2,256]{4,3,2,1,0:T(2,128)(2,1)} %param.13) | copy-start | bytes 1572868
  18.3 3.1 %copy-start.11 = (bf16[1,2,512,2,256]{4,3,2,1,0:T(2,128)(2,1)S(1)}, bf16[1,2,512,2,256]{4,3,2,1,0:T(2,128)(2,1)}, u32[]{:S(2)}) copy-start(bf16[1,2,512,2,256]{4,3,2,1,0:T(2,128)(2,1)} %param.12) | copy-start | bytes 3145732
  18.3 29.0 %collective-permute-start.2 = (bf16[1,2,448,2,256]{4,3,2,1,0:T(2,128)(2,1)S(1)}, bf16[1,2,448,2,256]{4,3,2,1,0:T(2,128)(2,1)S(1)}, u32[]{:S(2)}, u32[]{:S(2)}) collective-permute-start(bf16[1,2,448,2,256]{4,3,2,1,0:T(2,128)(2,1)S(1)} %get-tuple-element.18), channel_id=1, source_target_pairs={{256,0},{264,8},{272,16},{280,24},{288,32},{296,40},{304,48},{312,... | collective-permute-start | bytes 2752520 | tf_op jit(solution)/shard_map/ppermute | solution.py:25
  21.6 1.0 %copy-start.9 = (bf16[1,2,512,256]{3,2,1,0:T(8,128)(2,1)S(1)}, bf16[1,2,512,256]{3,2,1,0:T(8,128)(2,1)}, u32[]{:S(2)}) copy-start(bf16[1,2,512,256]{3,2,1,0:T(8,128)(2,1)} %q.1) | copy-start | bytes 1572868
  21.6 1.0 %copy-start.10 = (bf16[256,64]{0,1:T(8,128)(2,1)S(1)}, bf16[256,64]{0,1:T(8,128)(2,1)}, u32[]{:S(2)}) copy-start(bf16[256,64]{0,1:T(8,128)(2,1)} %param.14) | copy-start | bytes 98308
  22.6 23.3 %copy-start.7 = (s32[64,2]{0,1:T(2,128)S(1)}, s32[64,2]{0,1:T(2,128)}, u32[]{:S(2)}) copy-start(s32[64,2]{0,1:T(2,128)} %param.19) | copy-start | bytes 1540
  22.6 23.4 %copy-start.8 = (s32[64]{0:T(128)S(1)}, s32[64]{0:T(128)}, u32[]{:S(2)}) copy-start(s32[64]{0:T(128)} %requests.1) | copy-start | bytes 772
  31.2 14.8 %copy-start.5 = (f32[1,2,64,64]{3,2,1,0:T(8,128)S(1)}, f32[1,2,64,64]{3,2,1,0:T(8,128)}, u32[]{:S(2)}) copy-start(f32[1,2,64,64]{3,2,1,0:T(8,128)} %latent.1) | copy-start | bytes 98308
  45.9 1.4 %copy-start.3 = (s32[64,2,64]{2,1,0:T(2,128)S(1)}, s32[64,2,64]{2,1,0:T(2,128)}, u32[]{:S(2)}) copy-start(s32[64,2,64]{2,1,0:T(2,128)} %lists.5) | copy-start | bytes 98308
  47.3 0.8 %copy-start.4 = (f32[1,2,64,64]{3,2,1,0:T(8,128)S(1)}, f32[1,2,64,64]{3,2,1,0:T(8,128)}, u32[]{:S(2)}) copy-start(f32[1,2,64,64]{3,2,1,0:T(8,128)} %get-tuple-element.11.after) | copy-start | bytes 98308

commit v2 on v1

v2 whole, which is shorter than its diff:
```python
import math

import jax
import jax.numpy as jnp
from jax import lax
from jax.experimental.layout import Layout, with_layout_constraint
from jax.experimental import pallas as pl
from jax.experimental.pallas import tpu as pltpu
from jax.sharding import PartitionSpec as P

HD = 128
TILE = 128
SCALE = math.log2(math.e) / math.sqrt(HD)
VMEM = pltpu.MemorySpace.VMEM
SMEM = pltpu.MemorySpace.SMEM
HBM = pltpu.MemorySpace.HBM


def whole(space):
    return pl.BlockSpec(memory_space=space)


def from_behind(block, axis, distance):
    devices = range(lax.axis_size(axis))
    route = [((i - distance) % len(devices), i) for i in devices]
    return lax.ppermute(block, axis, route)


def counted(mask, axis):
    return jnp.sum(jnp.where(mask, 1.0, 0.0), axis=axis, keepdims=True)


def exchange_rows(listed_row, rows):
    n = listed_row.shape[1]
    keep = float(rows - n)
    down = lax.broadcasted_iota(jnp.int32, (n, n), 0).astype(jnp.float32)
    along = lax.broadcasted_iota(jnp.int32, (n, n), 1).astype(jnp.float32)
    diagonal = down == along
    listed_col = jnp.sum(
        jnp.where(diagonal, listed_row, 0.0), axis=1, keepdims=True
    )
    used_row = counted(listed_col == along + keep, 0)
    used_col = counted(listed_row == down + keep, 1)
    free_rank = jnp.sum(
        jnp.where(down < along, 1.0 - used_col, 0.0), axis=0, keepdims=True
    )
    low_rank = counted(jnp.logical_and(along < down, listed_row < keep), 1)
    match = jnp.logical_and(low_rank == free_rank, used_row == 0.0)
    found = jnp.sum(jnp.where(match, along + keep, 0.0), axis=1, keepdims=True)
    found = jnp.where(listed_col < keep, found, listed_col)
    found_row = jnp.sum(jnp.where(diagonal, found, 0.0), axis=0, keepdims=True)
    return listed_col, found_row


def pack_kernel(
    lists, fresh, early, bulk, held, mine, plan, where, list_sem, plan_sem, in_sem, out_sem
):
    _, slots, rows, _, _ = fresh.shape
    listed = early.shape[2]
    keep = rows - listed
    step = 8
    group = lax.axis_index("grp")
    load_list = pltpu.make_async_copy(lists.at[group], mine, list_sem)
    load_list.start()
    loads = [
        pltpu.make_async_copy(fresh.at[0, s], held.at[s], in_sem.at[s])
        for s in range(slots)
    ]
    for load in loads:
        load.start()
    load_list.wait()
    for s in range(slots):
        listed_row = mine[s : s + 1, :]
        _, found = exchange_rows(listed_row.astype(jnp.float32), rows)
        plan[2 * s : 2 * s + 1, :listed] = listed_row
        plan[2 * s + 1 : 2 * s + 2, :listed] = found.astype(jnp.int32)
    move = pltpu.make_async_copy(plan, where, plan_sem)
    move.start()
    move.wait()
    stores = []
    for s in range(slots):
        loads[s].wait()

        def exchange(i, carry, s=s):
            ids = [i * step + k for k in range(step)]
            at = [where[2 * s, j] for j in ids]
            to = [where[2 * s + 1, j] for j in ids]
            taken = [held[s, row] for row in at]
            given = [held[s, row] for row in to]
            for k in range(step):
                early[0, s, ids[k]] = taken[k]
            for k in range(step):
                held[s, at[k]] = given[k]
            return carry

        lax.fori_loop(0, listed // step, exchange, 0)
        store = pltpu.make_async_copy(
            held.at[s, pl.ds(0, keep)], bulk.at[0, s], out_sem.at[s]
        )
        store.start()
        stores.append(store)
    for store in stores:
        store.wait()


def pack(refresh_rows, fresh_kv):
    _, slots, rows, two, width = fresh_kv.shape
    listed = refresh_rows.shape[2]
    keep = rows - listed
    kv = fresh_kv.dtype
    return pl.pallas_call(
        pack_kernel,
        out_shape=(
            jax.ShapeDtypeStruct((1, slots, listed, two, width), kv),
            jax.ShapeDtypeStruct((1, slots, keep, two, width), kv),
        ),
        in_specs=[whole(HBM), whole(HBM)],
        out_specs=(whole(VMEM), whole(pl.ANY)),
        scratch_shapes=[
            pltpu.VMEM((slots, rows, two, width), kv),
            pltpu.VMEM((slots, listed), jnp.int32),
            pltpu.VMEM((8, TILE), jnp.int32),
            pltpu.SMEM((8, TILE), jnp.int32),
            pltpu.SemaphoreType.DMA,
            pltpu.SemaphoreType.DMA,
            pltpu.SemaphoreType.DMA((slots,)),
            pltpu.SemaphoreType.DMA((slots,)),
        ],
        compiler_params=pltpu.CompilerParams(vmem_limit_bytes=8 << 20),
        cost_estimate=pl.CostEstimate(
            flops=0, transcendentals=0, bytes_accessed=4 << 20
        ),
        name="pack",
    )(refresh_rows, fresh_kv)


def unpack_kernel(
    where,
    early,
    bulk,
    total,
    shown,
    step_size,
    latent,
    out,
    velocity,
    latent_next,
    held,
    v_held,
    in_sem,
    out_sem,
    v_sem,
):
    _, slots, rows, _, _ = out.shape
    ch = latent.shape[3]
    listed = early.shape[2]
    keep = rows - listed
    step = 8
    loads = [
        pltpu.make_async_copy(
            bulk.at[0, s], held.at[s, pl.ds(0, keep)], in_sem.at[s]
        )
        for s in range(slots)
    ]
    for load in loads:
        load.start()
    for s in range(slots):
        v = jnp.where(shown[s] > 0.0, total[:, s * ch : (s + 1) * ch], 0.0)
        v_held[0, s] = v
        v_held[1, s] = latent[0, s] + step_size[s] * v
    stores = [
        pltpu.make_async_copy(v_held.at[i], ref.at[0], v_sem.at[i])
        for i, ref in enumerate((velocity, latent_next))
    ]
    for store in stores:
        store.start()
    for s in range(slots):
        loads[s].wait()

        def place(i, carry, s=s):
            ids = [i * step + k for k in range(step)]
            at = [where[2 * s, j] for j in ids]
            to = [where[2 * s + 1, j] for j in ids]
            moved = [held[s, row] for row in at]
            new = [early[0, s, j] for j in ids]
            for k in range(step):
                held[s, to[k]] = moved[k]
            for k in range(step):
                held[s, at[k]] = new[k]
            return carry

        lax.fori_loop(0, listed // step, place, 0)
        store = pltpu.make_async_copy(held.at[s], out.at[0, s], out_sem.at[s])
        store.start()
        stores.append(store)
    for store in stores:
        store.wait()


def unpack(where, early, bulk, total, shown, step_size, latent):
    _, slots, listed, two, width = early.shape
    rows = bulk.shape[2] + listed
    kv = bulk.dtype
    return pl.pallas_call(
        unpack_kernel,
        out_shape=(
            jax.ShapeDtypeStruct((1, slots, rows, two, width), kv),
            jax.ShapeDtypeStruct(latent.shape, jnp.float32),
            jax.ShapeDtypeStruct(latent.shape, jnp.float32),
        ),
        in_specs=[whole(SMEM), whole(VMEM), whole(pl.ANY)] + [whole(VMEM)] * 4,
        out_specs=(whole(pl.ANY), whole(HBM), whole(HBM)),
        scratch_shapes=[
            pltpu.VMEM((slots, rows, two, width), kv),
            pltpu.VMEM((2,) + latent.shape[1:], jnp.float32),
            pltpu.SemaphoreType.DMA((slots,)),
            pltpu.SemaphoreType.DMA((slots,)),
            pltpu.SemaphoreType.DMA((2,)),
        ],
        compiler_params=pltpu.CompilerParams(vmem_limit_bytes=8 << 20),
        cost_estimate=pl.CostEstimate(
            flops=0, transcendentals=0, bytes_accessed=4 << 20
        ),
        name="unpack",
    )(where, early, bulk, total, shown, step_size, latent)


def prepare_kernel(
    lists, live, requests, times, bias, where, shown, step, theirs, list_sem
):
    slots = bias.shape[0]
    listed = lists.shape[2]
    rows = (bias.shape[2] - TILE) // 2
    groups = lax.axis_size("grp")
    group = lax.axis_index("grp")
    partner = lax.rem(group + groups // 2, groups)
    load_list = pltpu.make_async_copy(lists.at[partner], theirs, list_sem)
    load_list.start()
    ids = lax.broadcasted_iota(jnp.int32, (1, rows), 1)
    ids_down = lax.broadcasted_iota(jnp.int32, (listed, rows), 1).astype(jnp.float32)
    dead = jnp.float32(-jnp.inf)
    load_list.wait()
    for s in range(slots):
        partner_live = live[s, partner]
        listed_row = theirs[s : s + 1, :]
        listed_col, found = exchange_rows(listed_row.astype(jnp.float32), rows)
        where[2 * s : 2 * s + 1, :listed] = listed_row
        where[2 * s + 1 : 2 * s + 2, :listed] = found.astype(jnp.int32)
        replaced = counted(ids_down == listed_col, 0) > 0.0
        counts = jnp.logical_and(ids < partner_live, jnp.logical_not(replaced))
        bias[s, :, :rows] = jnp.where(ids < live[s, group], 0.0, dead)
        bias[s, :, rows : 2 * rows] = jnp.where(counts, 0.0, dead)
        bias[s, :, 2 * rows :] = jnp.full((1, TILE), dead)
        bias[s, :, 2 * rows : 2 * rows + listed] = jnp.where(
            listed_row < partner_live, 0.0, dead
        )
    _, share, ch = shown.shape
    share_ids = lax.axis_index("tp") * share + lax.broadcasted_iota(
        jnp.int32, (share, ch), 0
    )
    pair = lax.rem(group, groups // 2)
    for s in range(slots):
        request = requests[pair * slots + s]
        gap = times[1, request] - times[0, request]
        shown[s] = jnp.where(share_ids < live[s, group], 1.0, 0.0)
        step[s] = jnp.full((share, ch), gap, jnp.int32).astype(jnp.float32) / 1000.0


def prepare(refresh_rows, live_t, request_list, times_t, rows, latent):
    _, slots, listed = refresh_rows.shape
    aside = jax.ShapeDtypeStruct(latent.shape[1:], jnp.float32)
    return pl.pallas_call(
        prepare_kernel,
        out_shape=(
            jax.ShapeDtypeStruct((slots, 1, 2 * rows + TILE), jnp.float32),
            jax.ShapeDtypeStruct((8, TILE), jnp.int32),
            aside,
            aside,
        ),
        in_specs=[whole(HBM), whole(SMEM), whole(SMEM), whole(SMEM)],
        out_specs=(whole(VMEM),) * 4,
        scratch_shapes=[
            pltpu.VMEM((slots, listed), jnp.int32),
            pltpu.SemaphoreType.DMA,
        ],
        compiler_params=pltpu.CompilerParams(vmem_limit_bytes=4 << 20),
        cost_estimate=pl.CostEstimate(
            flops=0, transcendentals=0, bytes_accessed=1 << 20
        ),
        name="prepare",
    )(refresh_rows, live_t, request_list, times_t)


def tiles(array):
    return [array[:, i : i + TILE] for i in range(0, array.shape[1], TILE)]


def attend_kernel(bias, q, own, stale, text, text_other, early, w_t, out, scores):
    slot = pl.program_id(0)
    rows = own.shape[2]
    heads = q.shape[3] // HD
    part_rows = scores.shape[1]
    ch = w_t.shape[0]
    blocks = (
        (own, 0, bias[0, :, :rows]),
        (stale, rows, bias[0, :, rows : 2 * rows]),
        (early, 2 * rows, bias[0, :, 2 * rows :]),
        (text, 2 * rows + TILE, None),
        (text_other, 2 * rows + TILE + text.shape[2], None),
    )

    def score(unit, place, block, top):
        head, first = unit
        kv, at, block_bias = block
        s = lax.dot_general(
            q[0, 0, first : first + part_rows, head * HD : (head + 1) * HD],
            kv[0, 0, :, head * HD : (head + 1) * HD],
            (((1,), (1,)), ((), ())),
            preferred_element_type=jnp.float32,
        )
        if block_bias is not None:
            s = s + block_bias
        scores[place, :, at : at + s.shape[1]] = s
        for tile in tiles(s):
            top = tile if top is None else jnp.maximum(top, tile)
        return top

    def weigh(unit, place, block, shift, total, blended):
        head, _ = unit
        kv, at, _ = block
        weights = jnp.exp2(
            scores[place, :, at : at + kv.shape[2]] * SCALE - shift
        )
        for tile in tiles(weights):
            total = tile if total is None else total + tile
        part = jnp.dot(
            weights.astype(jnp.bfloat16),
            kv[0, 1, :, head * HD : (head + 1) * HD],
            preferred_element_type=jnp.float32,
        )
        return total, part if blended is None else blended + part

    units = [
        (head, first)
        for first in range(0, rows, part_rows)
        for head in range(heads)
    ]
    top = None
    for block in blocks:
        top = score(units[0], 0, block, top)
    velocity = {}
    for i, unit in enumerate(units):
        shift = jnp.max(top, axis=1, keepdims=True) * SCALE
        top = total = blended = None
        for block in blocks:
            if i + 1 < len(units):
                top = score(units[i + 1], (i + 1) % 2, block, top)
            total, blended = weigh(unit, i % 2, block, shift, total, blended)
        total = jnp.sum(total, axis=1, keepdims=True)
        head, first = unit
        v = lax.dot_general(
            (blended / total).astype(jnp.bfloat16),
            w_t[:, head * HD : (head + 1) * HD],
            (((1,), (1,)), ((), ())),
            preferred_element_type=jnp.float32,
        )
        velocity[first] = v if first not in velocity else velocity[first] + v

    for s in range(2):

        @pl.when(slot == s)
        def _(s=s):
            for first, v in velocity.items():
                out[first : first + part_rows, s * ch : (s + 1) * ch] = v


def attend(bias, queries, own, stale, text, text_other, early, w_t):
    _, slots, rows, inner = queries.shape
    ch = w_t.shape[0]
    keys = sum(a.shape[2] for a in (own, stale, text, text_other, early))

    def kv_spec(a):
        return pl.BlockSpec((1, 2, a.shape[2], inner), lambda s: (s, 0, 0, 0))

    return pl.pallas_call(
        attend_kernel,
        grid=(slots,),
        out_shape=jax.ShapeDtypeStruct((rows, slots * ch), jnp.float32),
        in_specs=[
            pl.BlockSpec((1, 1, bias.shape[2]), lambda s: (s, 0, 0)),
            pl.BlockSpec((1, 1, rows, inner), lambda s: (0, s, 0, 0)),
            kv_spec(own),
            kv_spec(stale),
            kv_spec(text),
            kv_spec(text_other),
            kv_spec(early),
            pl.BlockSpec((ch, inner), lambda s: (0, 0)),
        ],
        out_specs=pl.BlockSpec((rows, slots * ch), lambda s: (0, 0)),
        scratch_shapes=[pltpu.VMEM((2, rows // 2, keys), jnp.float32)],
        compiler_params=pltpu.CompilerParams(vmem_limit_bytes=24 << 20),
        cost_estimate=pl.CostEstimate(
            flops=20 * slots * rows * keys * inner,
            transcendentals=slots * rows * keys * inner // HD,
            bytes_accessed=4 << 20,
        ),
        name="attend",
    )(bias, queries, own, stale, text, text_other, early, w_t)


def tp_sum_kernel(
    part, out, leaving, arrived, mine, crossing, other, send, recv, send2, recv2
):
    t = lax.axis_index("tp")
    x, half = t // 2, lax.rem(t, 2)
    sides = lax.axis_size("tp") // 2
    share = out.shape[0]
    pair = 2 * share
    peers = [lax.rem(x + d, sides) for d in range(1, sides)]
    across = x * 2 + 1 - half

    barrier = pltpu.get_barrier_semaphore()
    for peer in peers:
        pl.semaphore_signal(
            barrier,
            inc=1,
            device_id={"tp": peer * 2 + half},
            device_id_type=pl.DeviceIdType.MESH,
        )
    pl.semaphore_signal(
        barrier,
        inc=1,
        device_id={"tp": across},
        device_id_type=pl.DeviceIdType.MESH,
    )
    leaving[...] = part[...].astype(leaving.dtype)
    pl.semaphore_wait(barrier, sides)

    copies = []
    for i, peer in enumerate(peers):
        copy = pltpu.make_async_remote_copy(
            src_ref=leaving.at[pl.ds(pl.multiple_of(peer * pair, 16), pair)],
            dst_ref=arrived.at[i],
            send_sem=send.at[i],
            recv_sem=recv.at[i],
            device_id={"tp": peer * 2 + half},
            device_id_type=pl.DeviceIdType.MESH,
        )
        copy.start()
        copies.append(copy)
    total = part[pl.ds(pl.multiple_of(x * pair, 8), pair)]
    for i, copy in enumerate(copies):
        copy.wait_recv()
        total = total + arrived[i].astype(jnp.float32)
    mine[...] = total
    there = pl.multiple_of((1 - half) * share, 8)
    crossing[...] = mine[pl.ds(there, share)].astype(crossing.dtype)
    copy = pltpu.make_async_remote_copy(
        src_ref=crossing,
        dst_ref=other,
        send_sem=send2,
        recv_sem=recv2,
        device_id={"tp": across},
        device_id_type=pl.DeviceIdType.MESH,
    )
    copy.start()
    copy.wait_recv()
    here = pl.multiple_of(half * share, 8)
    out[...] = mine[pl.ds(here, share)] + other[...].astype(jnp.float32)
    for done in copies:
        done.wait_send()
    copy.wait_send()


def tp_sum(part, members):
    rows, width = part.shape
    share = rows // members
    sides = members // 2
    return pl.pallas_call(
        tp_sum_kernel,
        out_shape=jax.ShapeDtypeStruct((share, width), jnp.float32),
        in_specs=[whole(VMEM)],
        out_specs=whole(VMEM),
        scratch_shapes=[
            pltpu.VMEM((rows, width), jnp.bfloat16),
            pltpu.VMEM((sides - 1, 2 * share, width), jnp.bfloat16),
            pltpu.VMEM((2 * share, width), jnp.float32),
            pltpu.VMEM((share, width), jnp.bfloat16),
            pltpu.VMEM((share, width), jnp.bfloat16),
            pltpu.SemaphoreType.DMA((sides - 1,)),
            pltpu.SemaphoreType.DMA((sides - 1,)),
            pltpu.SemaphoreType.DMA,
            pltpu.SemaphoreType.DMA,
        ],
        compiler_params=pltpu.CompilerParams(
            collective_id=0, has_side_effects=True, vmem_limit_bytes=4 << 20
        ),
        cost_estimate=pl.CostEstimate(
            flops=0, transcendentals=0, bytes_accessed=4 << 20
        ),
        name="tp_sum",
    )(part)


def in_order(array):
    return with_layout_constraint(array, Layout(tuple(range(array.ndim))))


def apart(kv):
    return jnp.transpose(kv[0], (0, 2, 1, 3))


def shards(
    queries,
    fresh_kv,
    stale_kv,
    text_kv,
    w_velocity,
    latent,
    live_counts,
    refresh_rows,
    request_list,
    timesteps,
):
    half_groups = lax.axis_size("grp") // 2
    live_t = live_counts.T
    times_t = timesteps.T
    rows = fresh_kv.shape[2]
    listed = refresh_rows.shape[2]
    text_other = in_order(from_behind(in_order(text_kv), "grp", half_groups))
    early_out, bulk_out = pack(refresh_rows, fresh_kv)
    early = from_behind(early_out, "grp", half_groups)
    bias, where, shown, step_size = prepare(
        refresh_rows, live_t, request_list, times_t, rows, latent
    )
    text_other, bulk_out, bias, where = lax.optimization_barrier(
        (text_other, bulk_out, bias, where)
    )
    bulk = from_behind(bulk_out, "grp", half_groups)
    early_apart = jnp.pad(apart(early), ((0, 0), (0, 0), (0, TILE - listed), (0, 0)))
    part = attend(
        bias,
        queries,
        apart(fresh_kv),
        apart(stale_kv),
        apart(text_kv),
        apart(text_other),
        early_apart,
        w_velocity.T,
    )
    total = tp_sum(part, lax.axis_size("tp"))
    return unpack(where, early, bulk, total, shown, step_size, latent)


def solution(mesh):
    return jax.shard_map(
        shards,
        mesh=mesh,
        in_specs=(
            P("grp", None, None, "tp"),
            P("grp", None, None, None, "tp"),
            P("grp", None, None, None, "tp"),
            P("grp", None, None, None, "tp"),
            P("tp", None),
            P("grp", None, "tp", None),
            P(),
            P(),
            P(),
            P(),
        ),
        out_specs=(
            P("grp", None, None, None, "tp"),
            P("grp", None, "tp", None),
            P("grp", None, "tp", None),
        ),
        check_vma=False,
    )
```

time: 52.3 us -> 45.7 us (0.87)
  the two profiles are of different devices: /device:TPU:24 before, /device:TPU:6 now
where the time goes in v2:
time: 45.7 us; the launch traced here: 45.3 us
  Pallas kernels  25.6 us (56%)
  starting transfers between devices  9.45 us (21%)
  waiting for transfers between devices  5.26 us (12%)
  local copies, waits for them, and re-layouts  4.15 us (9%)
  between operations  0.84 us (2%)
    pallas_call x1, Pallas kernels, tp_sum(): pl.pallas_call(tp_sum_kernel, out_shape=jax.ShapeDtypeStruct((share, widt...  13.1 us
    ppermute x3, starting transfers between devices, from_behind(): return lax.ppermute(block, axis, route)  9.45 us
    pallas_call x1, Pallas kernels, attend(): pl.pallas_call(attend_kernel, grid=(slots,), out_shape=jax.ShapeDtypeStru...  6.7 us
    ppermute x3, waiting for transfers between devices, from_behind(): return lax.ppermute(block, axis, route)  5.26 us
    unnamed x26, local copies, waits for them, and re-layouts  4.06 us
    pallas_call x1, Pallas kernels, unpack(): pl.pallas_call(unpack_kernel, out_shape=(jax.ShapeDtypeStruct((1, slots,...  2.77 us
    pallas_call x1, Pallas kernels, pack(): pl.pallas_call(pack_kernel, out_shape=(jax.ShapeDtypeStruct((1, slots, li...  2.19 us
  transfers between devices with their start and end apart: 3, of which 1 were waited for; matrix products, arithmetic and copies ran while one was open for 1% of the time, Pallas kernels for 50%

profile of v2, /device:TPU:6, one launch (start us, length us, event | category | flops | bytes accessed | tf_op | source)
XLA Modules:
  0.0 45.3 jit_solution(8330383882746625165)
XLA Ops:
  0.6 3.5 %collective-permute-start = (bf16[1,2,256,2,256]{4,3,2,1,0:T(2,128)(2,1)}, bf16[1,2,256,2,256]{4,3,2,1,0:T(2,128)(2,1)S(1)}, u32[]{:S(2)}, u32[]{:S(2)}) collective-permute-start(bf16[1,2,256,2,256]{4,3,2,1,0:T(2,128)(2,1)} %param.13), channel_id=1, source_target_pairs={{256,0},{264,8},{272,16},{280,24},{288,32},{296,40},{304,48},{312,... | collective-permute-start | bytes 1572872 | tf_op jit(solution)/shard_map/ppermute | solution.py:26
  4.1 1.2 %copy-done = bf16[1,2,512,2,256]{4,3,2,1,0:T(2,128)(2,1)S(1)} copy-done((bf16[1,2,512,2,256]{4,3,2,1,0:T(2,128)(2,1)S(1)}, bf16[1,2,512,2,256]{4,3,2,1,0:T(2,128)(2,1)}, u32[]{:S(2)}) %copy-start) | copy-done | bytes 1048600
  5.4 0.8 %copy-done.2 = s32[64,2,64]{2,1,0:T(2,128)S(1)} copy-done((s32[64,2,64]{2,1,0:T(2,128)S(1)}, s32[64,2,64]{2,1,0:T(2,128)}, u32[]{:S(2)}) %copy-start.2) | copy-done | bytes 32792
  6.2 2.2 %pack.1 = (bf16[1,2,64,2,256]{4,3,2,1,0:T(2,128)(2,1)S(1)}, bf16[1,2,448,2,256]{4,3,2,1,0:T(2,128)(2,1)S(1)}) custom-call(s32[64,2,64]{2,1,0:T(2,128)S(1)} %copy-done.2, bf16[1,2,512,2,256]{4,3,2,1,0:T(2,128)(2,1)S(1)} %copy-done), custom_call_target="tpu_custom_call" | custom-call | bytes 4194304 | tf_op jit(solution)/shard_map/pack/pallas_call | solution.py:111
  8.4 2.4 %collective-permute-start.1 = (bf16[1,2,64,2,256]{4,3,2,1,0:T(2,128)(2,1)S(1)}, bf16[1,2,64,2,256]{4,3,2,1,0:T(2,128)(2,1)S(1)}, u32[]{:S(2)}, u32[]{:S(2)}) collective-permute-start(bf16[1,2,64,2,256]{4,3,2,1,0:T(2,128)(2,1)S(1)} %get-tuple-element.17), channel_id=1, source_target_pairs={{256,0},{264,8},{272,16},{280,24},{288,32},{296,40},{304,48},{312,... | collective-permute-start | bytes 393224 | tf_op jit(solution)/shard_map/ppermute | solution.py:26
  10.8 0.0 copy-start.4
  10.8 0.0 copy-start.6
  10.8 0.6 %copy-done.4 = s32[64,2]{0,1:T(2,128)S(1)} copy-done((s32[64,2]{0,1:T(2,128)S(1)}, s32[64,2]{0,1:T(2,128)}, u32[]{:S(2)}) %copy-start.4) | copy-done | bytes 536
  11.4 0.8 %prepare.1 = (f32[2,1,1152]{2,1,0:T(1,128)S(1)}, s32[8,128]{1,0:T(8,128)S(1)}, f32[2,64,64]{2,1,0:T(8,128)S(1)}, f32[2,64,64]{2,1,0:T(8,128)S(1)}) custom-call(s32[64,2,64]{2,1,0:T(2,128)S(1)} %copy-done.2, s32[2,64]{1,0:T(2,128)S(1)} %bitcast.31, s32[64]{0:T(128)S(1)} %copy-done.6, s32[2,64]{1,0:T(2,128)S(1)} %bitcast.32), custom_call_target="tpu_custom_call" | custom-call | bytes 1048576 | tf_op jit(solution)/shard_map/prepare/pallas_call | solution.py:272
  12.3 5.3 %collective-permute-done = bf16[1,2,256,2,256]{4,3,2,1,0:T(2,128)(2,1)S(1)} collective-permute-done((bf16[1,2,256,2,256]{4,3,2,1,0:T(2,128)(2,1)}, bf16[1,2,256,2,256]{4,3,2,1,0:T(2,128)(2,1)S(1)}, u32[]{:S(2)}, u32[]{:S(2)}) %collective-permute-start) | collective-permute-done | bytes 524320 | tf_op jit(solution)/shard_map/ppermute | solution.py:26
  17.6 3.6 %collective-permute-start.2 = (bf16[1,2,448,2,256]{4,3,2,1,0:T(2,128)(2,1)S(1)}, bf16[1,2,448,2,256]{4,3,2,1,0:T(2,128)(2,1)S(1)}, u32[]{:S(2)}, u32[]{:S(2)}) collective-permute-start(bf16[1,2,448,2,256]{4,3,2,1,0:T(2,128)(2,1)S(1)} %get-tuple-element.18), channel_id=1, source_target_pairs={{256,0},{264,8},{272,16},{280,24},{288,32},{296,40},{304,48},{312,... | collective-permute-start | bytes 2752520 | tf_op jit(solution)/shard_map/ppermute | solution.py:26
  21.2 0.1 copy.24
  21.3 0.1 copy.26
  21.4 0.1 copy.23
  21.6 0.0 collective-permute-done.1.early
  21.6 0.0 copy-start.7
  21.6 0.0 copy-start.8
  21.7 0.1 copy.25
  21.7 0.9 %copy-done.7 = bf16[1,2,512,256]{3,2,1,0:T(8,128)(2,1)S(1)} copy-done((bf16[1,2,512,256]{3,2,1,0:T(8,128)(2,1)S(1)}, bf16[1,2,512,256]{3,2,1,0:T(8,128)(2,1)}, u32[]{:S(2)}) %copy-start.7) | copy-done | bytes 524312
  22.7 6.7 %attend.1.part = f32[512,128]{1,0:T(8,128)S(1)} custom-call(f32[2,1,1152]{2,1,0:T(1,128)S(1)} %get-tuple-element.19.bias, bf16[1,2,512,256]{3,2,1,0:T(8,128)(2,1)S(1)} %copy-done.7, bf16[2,2,512,256]{3,2,1,0:T(8,128)(2,1)S(1)} %bitcast.26, bf16[2,2,512,256]{3,2,1,0:T(8,128)(2,1)S(1)} %bitcast.27, bf16[2,2,256,256]{3,2,1,0:T(8,128)(2,1)S(1)} %bitcast.29, ...), custom_call_target="tpu_custom_call" | custom-call | flops 8724152320 | bytes 4194304 | tf_op jit(solution)/shard_map/attend/pallas_call | solution.py:385
  29.4 0.0 copy-start.3
  29.4 13.1 %tp_sum.1.total = f32[64,128]{1,0:T(8,128)S(1)} custom-call(f32[512,128]{1,0:T(8,128)S(1)} %attend.1.part), custom_call_target="tpu_custom_call" | custom-call | bytes 4194304 | tf_op jit(solution)/shard_map/tp_sum/pallas_call | solution.py:479
  42.5 0.0 collective-permute-done.2.bulk
  42.5 2.8 %unpack.1 = (bf16[1,2,512,2,256]{4,3,2,1,0:T(2,128)(2,1)}, f32[1,2,64,64]{3,2,1,0:T(8,128)}, f32[1,2,64,64]{3,2,1,0:T(8,128)}) custom-call(s32[8,128]{1,0:T(8,128)S(1)} %get-tuple-element.16.where, bf16[1,2,64,2,256]{4,3,2,1,0:T(2,128)(2,1)S(1)} %collective-permute-done.1.early, bf16[1,2,448,2,256]{4,3,2,1,0:T(2,128)(2,1)S(1)} %collective-permute-done.2.bulk, ...), custom_call_target="tpu_custom_call" | custom-call | bytes 4194304 | tf_op jit(solution)/shard_map/unpack/pallas_call | solution.py:204
  (15 shorter events, 0.1 us)
Async XLA Ops:
  0.6 16.9 %collective-permute-start = (bf16[1,2,256,2,256]{4,3,2,1,0:T(2,128)(2,1)}, bf16[1,2,256,2,256]{4,3,2,1,0:T(2,128)(2,1)S(1)}, u32[]{:S(2)}, u32[]{:S(2)}) collective-permute-start(bf16[1,2,256,2,256]{4,3,2,1,0:T(2,128)(2,1)} %param.13), channel_id=1, source_target_pairs={{256,0},{264,8},{272,16},{280,24},{288,32},{296,40},{304,48},{312,... | collective-permute-start | bytes 1572872 | tf_op jit(solution)/shard_map/ppermute | solution.py:26
  4.1 1.2 %copy-start = (bf16[1,2,512,2,256]{4,3,2,1,0:T(2,128)(2,1)S(1)}, bf16[1,2,512,2,256]{4,3,2,1,0:T(2,128)(2,1)}, u32[]{:S(2)}) copy-start(bf16[1,2,512,2,256]{4,3,2,1,0:T(2,128)(2,1)} %fresh.1) | copy-start | bytes 3145732
  5.4 0.8 %copy-start.2 = (s32[64,2,64]{2,1,0:T(2,128)S(1)}, s32[64,2,64]{2,1,0:T(2,128)}, u32[]{:S(2)}) copy-start(s32[64,2,64]{2,1,0:T(2,128)} %lists.3) | copy-start | bytes 98308
  6.2 4.6 %copy-start.5 = (s32[64,2]{0,1:T(2,128)S(1)}, s32[64,2]{0,1:T(2,128)}, u32[]{:S(2)}) copy-start(s32[64,2]{0,1:T(2,128)} %param.19) | copy-start | bytes 1540
  6.2 15.0 %copy-start.1 = (bf16[1,2,512,2,256]{4,3,2,1,0:T(2,128)(2,1)S(1)}, bf16[1,2,512,2,256]{4,3,2,1,0:T(2,128)(2,1)}, u32[]{:S(2)}) copy-start(bf16[1,2,512,2,256]{4,3,2,1,0:T(2,128)(2,1)} %fresh.1) | copy-start | bytes 3145732
  8.4 13.2 %collective-permute-start.1 = (bf16[1,2,64,2,256]{4,3,2,1,0:T(2,128)(2,1)S(1)}, bf16[1,2,64,2,256]{4,3,2,1,0:T(2,128)(2,1)S(1)}, u32[]{:S(2)}, u32[]{:S(2)}) collective-permute-start(bf16[1,2,64,2,256]{4,3,2,1,0:T(2,128)(2,1)S(1)} %get-tuple-element.17), channel_id=1, source_target_pairs={{256,0},{264,8},{272,16},{280,24},{288,32},{296,40},{304,48},{312,... | collective-permute-start | bytes 393224 | tf_op jit(solution)/shard_map/ppermute | solution.py:26
  10.8 0.7 %copy-start.4 = (s32[64,2]{0,1:T(2,128)S(1)}, s32[64,2]{0,1:T(2,128)}, u32[]{:S(2)}) copy-start(s32[64,2]{0,1:T(2,128)} %param.16) | copy-start | bytes 1540
  10.8 0.7 %copy-start.6 = (s32[64]{0:T(128)S(1)}, s32[64]{0:T(128)}, u32[]{:S(2)}) copy-start(s32[64]{0:T(128)} %requests.1) | copy-start | bytes 772
  17.5 3.8 %copy-start.10 = (bf16[1,2,256,2,256]{4,3,2,1,0:T(2,128)(2,1)S(1)}, bf16[1,2,256,2,256]{4,3,2,1,0:T(2,128)(2,1)}, u32[]{:S(2)}) copy-start(bf16[1,2,256,2,256]{4,3,2,1,0:T(2,128)(2,1)} %param.13) | copy-start | bytes 1572868
  17.5 3.9 %copy-start.9 = (bf16[1,2,512,2,256]{4,3,2,1,0:T(2,128)(2,1)S(1)}, bf16[1,2,512,2,256]{4,3,2,1,0:T(2,128)(2,1)}, u32[]{:S(2)}) copy-start(bf16[1,2,512,2,256]{4,3,2,1,0:T(2,128)(2,1)} %param.12) | copy-start | bytes 3145732
  17.6 25.0 %collective-permute-start.2 = (bf16[1,2,448,2,256]{4,3,2,1,0:T(2,128)(2,1)S(1)}, bf16[1,2,448,2,256]{4,3,2,1,0:T(2,128)(2,1)S(1)}, u32[]{:S(2)}, u32[]{:S(2)}) collective-permute-start(bf16[1,2,448,2,256]{4,3,2,1,0:T(2,128)(2,1)S(1)} %get-tuple-element.18), channel_id=1, source_target_pairs={{256,0},{264,8},{272,16},{280,24},{288,32},{296,40},{304,48},{312,... | collective-permute-start | bytes 2752520 | tf_op jit(solution)/shard_map/ppermute | solution.py:26
  21.6 1.0 %copy-start.7 = (bf16[1,2,512,256]{3,2,1,0:T(8,128)(2,1)S(1)}, bf16[1,2,512,256]{3,2,1,0:T(8,128)(2,1)}, u32[]{:S(2)}) copy-start(bf16[1,2,512,256]{3,2,1,0:T(8,128)(2,1)} %q.1) | copy-start | bytes 1572868
  21.6 1.0 %copy-start.8 = (bf16[256,64]{0,1:T(8,128)(2,1)S(1)}, bf16[256,64]{0,1:T(8,128)(2,1)}, u32[]{:S(2)}) copy-start(bf16[256,64]{0,1:T(8,128)(2,1)} %param.14) | copy-start | bytes 98308
  29.4 13.1 %copy-start.3 = (f32[1,2,64,64]{3,2,1,0:T(8,128)S(1)}, f32[1,2,64,64]{3,2,1,0:T(8,128)}, u32[]{:S(2)}) copy-start(f32[1,2,64,64]{3,2,1,0:T(8,128)} %latent.1) | copy-start | bytes 98308

commit v3 on v2

--- a/solution.py
+++ b/solution.py
@@ -134,25 +134,9 @@
     )(refresh_rows, fresh_kv)
 
 
-def unpack_kernel(
-    where,
-    early,
-    bulk,
-    total,
-    shown,
-    step_size,
-    latent,
-    out,
-    velocity,
-    latent_next,
-    held,
-    v_held,
-    in_sem,
-    out_sem,
-    v_sem,
-):
+def unpack_kernel(where, early, bulk, out, passed, held, in_sem, out_sem):
+    passed[...] = jnp.zeros_like(passed)
     _, slots, rows, _, _ = out.shape
-    ch = latent.shape[3]
     listed = early.shape[2]
     keep = rows - listed
     step = 8
@@ -164,16 +148,7 @@
     ]
     for load in loads:
         load.start()
-    for s in range(slots):
-        v = jnp.where(shown[s] > 0.0, total[:, s * ch : (s + 1) * ch], 0.0)
-        v_held[0, s] = v
-        v_held[1, s] = latent[0, s] + step_size[s] * v
-    stores = [
-        pltpu.make_async_copy(v_held.at[i], ref.at[0], v_sem.at[i])
-        for i, ref in enumerate((velocity, latent_next))
-    ]
-    for store in stores:
-        store.start()
+    stores = []
     for s in range(slots):
         loads[s].wait()
 
@@ -197,7 +172,7 @@
         store.wait()
 
 
-def unpack(where, early, bulk, total, shown, step_size, latent):
+def unpack(where, early, bulk):
     _, slots, listed, two, width = early.shape
     rows = bulk.shape[2] + listed
     kv = bulk.dtype
@@ -205,24 +180,44 @@
         unpack_kernel,
         out_shape=(
             jax.ShapeDtypeStruct((1, slots, rows, two, width), kv),
-            jax.ShapeDtypeStruct(latent.shape, jnp.float32),
-            jax.ShapeDtypeStruct(latent.shape, jnp.float32),
-        ),
-        in_specs=[whole(SMEM), whole(VMEM), whole(pl.ANY)] + [whole(VMEM)] * 4,
-        out_specs=(whole(pl.ANY), whole(HBM), whole(HBM)),
+            jax.ShapeDtypeStruct((8, TILE), jnp.float32),
+        ),
+        in_specs=[whole(SMEM), whole(VMEM), whole(pl.ANY)],
+        out_specs=(whole(pl.ANY), whole(VMEM)),
         scratch_shapes=[
             pltpu.VMEM((slots, rows, two, width), kv),
-            pltpu.VMEM((2,) + latent.shape[1:], jnp.float32),
             pltpu.SemaphoreType.DMA((slots,)),
             pltpu.SemaphoreType.DMA((slots,)),
-            pltpu.SemaphoreType.DMA((2,)),
         ],
         compiler_params=pltpu.CompilerParams(vmem_limit_bytes=8 << 20),
         cost_estimate=pl.CostEstimate(
             flops=0, transcendentals=0, bytes_accessed=4 << 20
         ),
         name="unpack",
-    )(where, early, bulk, total, shown, step_size, latent)
+    )(where, early, bulk)
+
+
+def finish_kernel(kept, other, shown, step_size, latent, after, velocity, latent_next):
+    _, slots, _, ch = latent.shape
+    total = kept[...] + other[...].astype(jnp.float32)
+    for s in range(slots):
+        v = jnp.where(shown[s] > 0.0, total[:, s * ch : (s + 1) * ch], 0.0)
+        velocity[0, s] = v
+        latent_next[0, s] = latent[0, s] + step_size[s] * v
+
+
+def finish(kept, other, shown, step_size, latent, after):
+    return pl.pallas_call(
+        finish_kernel,
+        out_shape=(jax.ShapeDtypeStruct(latent.shape, jnp.float32),) * 2,
+        in_specs=[whole(VMEM)] * 6,
+        out_specs=(whole(VMEM),) * 2,
+        compiler_params=pltpu.CompilerParams(vmem_limit_bytes=4 << 20),
+        cost_estimate=pl.CostEstimate(
+            flops=0, transcendentals=0, bytes_accessed=1 << 18
+        ),
+        name="finish",
+    )(kept, other, shown, step_size, latent, after)
 
 
 def prepare_kernel(
@@ -295,8 +290,54 @@
     return [array[:, i : i + TILE] for i in range(0, array.shape[1], TILE)]
 
 
-def attend_kernel(bias, q, own, stale, text, text_other, early, w_t, out, scores):
+def attend_kernel(
+    bias,
+    q,
+    own,
+    stale,
+    text,
+    text_other,
+    early,
+    w_t,
+    kept,
+    away,
+    scores,
+    packed,
+    leaving,
+    arrived,
+    send,
+    recv,
+):
     slot = pl.program_id(0)
+    t = lax.axis_index("tp")
+    x, half = t // 2, lax.rem(t, 2)
+    sides = lax.axis_size("tp") // 2
+    share = kept.shape[0]
+    peers = [lax.rem(x + d, sides) * 2 + half for d in range(1, sides)]
+
+    def along_x(s, i):
+        at = pl.multiple_of(peers[i] // 2 * share, share)
+        return pltpu.make_async_remote_copy(
+            src_ref=leaving.at[s, pl.ds(at, share)],
+            dst_ref=arrived.at[s, i],
+            send_sem=send.at[s, i],
+            recv_sem=recv.at[s, i],
+            device_id={"tp": peers[i]},
+            device_id_type=pl.DeviceIdType.MESH,
+        )
+
+    barrier = pltpu.get_barrier_semaphore()
+
+    @pl.when(slot == 0)
+    def _():
+        for peer in peers:
+            pl.semaphore_signal(
+                barrier,
+                inc=1,
+                device_id={"tp": peer},
+                device_id_type=pl.DeviceIdType.MESH,
+            )
+
     rows = own.shape[2]
     heads = q.shape[3] // HD
     part_rows = scores.shape[1]
@@ -366,18 +407,44 @@
         )
         velocity[first] = v if first not in velocity else velocity[first] + v
 
-    for s in range(2):
-
-        @pl.when(slot == s)
-        def _(s=s):
-            for first, v in velocity.items():
-                out[first : first + part_rows, s * ch : (s + 1) * ch] = v
-
-
-def attend(bias, queries, own, stale, text, text_other, early, w_t):
+    for first, v in velocity.items():
+        for at in range(0, part_rows, 2 * share):
+            both = jnp.concatenate(
+                [v[at : at + share], v[at + share : at + 2 * share]], axis=1
+            )
+            to = (first + at) // 2
+            packed[slot, to : to + share] = both
+            leaving[slot, to : to + share] = both.astype(leaving.dtype)
+
+    @pl.when(slot == 0)
+    def _():
+        pl.semaphore_wait(barrier, sides - 1)
+
+    for i in range(sides - 1):
+        along_x(slot, i).start()
+
+    @pl.when(slot == pl.num_programs(0) - 1)
+    def _():
+        for s in range(arrived.shape[0]):
+            total = packed[s, pl.ds(pl.multiple_of(x * share, share), share)]
+            for i in range(sides - 1):
+                along_x(s, i).wait_recv()
+                total = total + arrived[s, i].astype(jnp.float32)
+            low, high = total[:, :ch], total[:, ch:]
+            lanes = slice(s * ch, (s + 1) * ch)
+            kept[:, lanes] = jnp.where(half == 0, low, high)
+            away[:, lanes] = jnp.where(half == 0, high, low).astype(away.dtype)
+        for s in range(arrived.shape[0]):
+            for i in range(sides - 1):
+                along_x(s, i).wait_send()
+
+
+def attend(bias, queries, own, stale, text, text_other, early, w_t, members):
     _, slots, rows, inner = queries.shape
     ch = w_t.shape[0]
     keys = sum(a.shape[2] for a in (own, stale, text, text_other, early))
+    share, sides = rows // members, members // 2
+    sent = jnp.bfloat16
 
     def kv_spec(a):
         return pl.BlockSpec((1, 2, a.shape[2], inner), lambda s: (s, 0, 0, 0))
@@ -385,7 +452,10 @@
     return pl.pallas_call(
         attend_kernel,
         grid=(slots,),
-        out_shape=jax.ShapeDtypeStruct((rows, slots * ch), jnp.float32),
+        out_shape=(
+            jax.ShapeDtypeStruct((share, slots * ch), jnp.float32),
+            jax.ShapeDtypeStruct((share, slots * ch), sent),
+        ),
         in_specs=[
             pl.BlockSpec((1, 1, bias.shape[2]), lambda s: (s, 0, 0)),
             pl.BlockSpec((1, 1, rows, inner), lambda s: (0, s, 0, 0)),
@@ -396,110 +466,25 @@
             kv_spec(early),
             pl.BlockSpec((ch, inner), lambda s: (0, 0)),
         ],
-        out_specs=pl.BlockSpec((rows, slots * ch), lambda s: (0, 0)),
-        scratch_shapes=[pltpu.VMEM((2, rows // 2, keys), jnp.float32)],
-        compiler_params=pltpu.CompilerParams(vmem_limit_bytes=24 << 20),
+        out_specs=(pl.BlockSpec((share, slots * ch), lambda s: (0, 0)),) * 2,
+        scratch_shapes=[
+            pltpu.VMEM((2, rows // 2, keys), jnp.float32),
+            pltpu.VMEM((slots, rows // 2, 2 * ch), jnp.float32),
+            pltpu.VMEM((slots, rows // 2, 2 * ch), sent),
+            pltpu.VMEM((slots, sides - 1, share, 2 * ch), sent),
+            pltpu.SemaphoreType.DMA((slots, sides - 1)),
+            pltpu.SemaphoreType.DMA((slots, sides - 1)),
+        ],
+        compiler_params=pltpu.CompilerParams(
+            collective_id=0, has_side_effects=True, vmem_limit_bytes=24 << 20
+        ),
         cost_estimate=pl.CostEstimate(
-            flops=20 * slots * rows * keys * inner,
+            flops=40 * slots * rows * keys * inner,
             transcendentals=slots * rows * keys * inner // HD,
             bytes_accessed=4 << 20,
         ),
         name="attend",
     )(bias, queries, own, stale, text, text_other, early, w_t)
-
-
-def tp_sum_kernel(
-    part, out, leaving, arrived, mine, crossing, other, send, recv, send2, recv2
-):
-    t = lax.axis_index("tp")
-    x, half = t // 2, lax.rem(t, 2)
-    sides = lax.axis_size("tp") // 2
-    share = out.shape[0]
-    pair = 2 * share
-    peers = [lax.rem(x + d, sides) for d in range(1, sides)]
-    across = x * 2 + 1 - half
-
-    barrier = pltpu.get_barrier_semaphore()
-    for peer in peers:
-        pl.semaphore_signal(
-            barrier,
-            inc=1,
-            device_id={"tp": peer * 2 + half},
-            device_id_type=pl.DeviceIdType.MESH,
-        )
-    pl.semaphore_signal(
-        barrier,
-        inc=1,
-        device_id={"tp": across},
-        device_id_type=pl.DeviceIdType.MESH,
-    )
-    leaving[...] = part[...].astype(leaving.dtype)
-    pl.semaphore_wait(barrier, sides)
-
-    copies = []
-    for i, peer in enumerate(peers):
-        copy = pltpu.make_async_remote_copy(
-            src_ref=leaving.at[pl.ds(pl.multiple_of(peer * pair, 16), pair)],
-            dst_ref=arrived.at[i],
-            send_sem=send.at[i],
-            recv_sem=recv.at[i],
-            device_id={"tp": peer * 2 + half},
-            device_id_type=pl.DeviceIdType.MESH,
-        )
-        copy.start()
-        copies.append(copy)
-    total = part[pl.ds(pl.multiple_of(x * pair, 8), pair)]
-    for i, copy in enumerate(copies):
-        copy.wait_recv()
-        total = total + arrived[i].astype(jnp.float32)
-    mine[...] = total
-    there = pl.multiple_of((1 - half) * share, 8)
-    crossing[...] = mine[pl.ds(there, share)].astype(crossing.dtype)
-    copy = pltpu.make_async_remote_copy(
-        src_ref=crossing,
-        dst_ref=other,
-        send_sem=send2,
-        recv_sem=recv2,
-        device_id={"tp": across},
-        device_id_type=pl.DeviceIdType.MESH,
-    )
-    copy.start()
-    copy.wait_recv()
-    here = pl.multiple_of(half * share, 8)
-    out[...] = mine[pl.ds(here, share)] + other[...].astype(jnp.float32)
-    for done in copies:
-        done.wait_send()
-    copy.wait_send()
-
-
-def tp_sum(part, members):
-    rows, width = part.shape
-    share = rows // members
-    sides = members // 2
-    return pl.pallas_call(
-        tp_sum_kernel,
-        out_shape=jax.ShapeDtypeStruct((share, width), jnp.float32),
-        in_specs=[whole(VMEM)],
-        out_specs=whole(VMEM),
-        scratch_shapes=[
-            pltpu.VMEM((rows, width), jnp.bfloat16),
-            pltpu.VMEM((sides - 1, 2 * share, width), jnp.bfloat16),
-            pltpu.VMEM((2 * share, width), jnp.float32),
-            pltpu.VMEM((share, width), jnp.bfloat16),
-            pltpu.VMEM((share, width), jnp.bfloat16),
-            pltpu.SemaphoreType.DMA((sides - 1,)),
-            pltpu.SemaphoreType.DMA((sides - 1,)),
-            pltpu.SemaphoreType.DMA,
-            pltpu.SemaphoreType.DMA,
-        ],
-        compiler_params=pltpu.CompilerParams(
-            collective_id=0, has_side_effects=True, vmem_limit_bytes=4 << 20
-        ),
-        cost_estimate=pl.CostEstimate(
-            flops=0, transcendentals=0, bytes_accessed=4 << 20
-        ),
-        name="tp_sum",
-    )(part)
 
 
 def in_order(array):
@@ -529,16 +514,14 @@
     listed = refresh_rows.shape[2]
     text_other = in_order(from_behind(in_order(text_kv), "grp", half_groups))
     early_out, bulk_out = pack(refresh_rows, fresh_kv)
-    early = from_behind(early_out, "grp", half_groups)
+    early = in_order(from_behind(in_order(early_out), "grp", half_groups))
     bias, where, shown, step_size = prepare(
         refresh_rows, live_t, request_list, times_t, rows, latent
     )
-    text_other, bulk_out, bias, where = lax.optimization_barrier(
-        (text_other, bulk_out, bias, where)
-    )
+    bulk_out, bias, where = lax.optimization_barrier((bulk_out, bias, where))
     bulk = from_behind(bulk_out, "grp", half_groups)
     early_apart = jnp.pad(apart(early), ((0, 0), (0, 0), (0, TILE - listed), (0, 0)))
-    part = attend(
+    kept, away = attend(
         bias,
         queries,
         apart(fresh_kv),
@@ -547,9 +530,15 @@
         apart(text_other),
         early_apart,
         w_velocity.T,
-    )
-    total = tp_sum(part, lax.axis_size("tp"))
-    return unpack(where, early, bulk, total, shown, step_size, latent)
+        lax.axis_size("tp"),
+    )
+    members = range(lax.axis_size("tp"))
+    other = lax.ppermute(away, "tp", [(i, i ^ 1) for i in members])
+    next_stale, passed = unpack(where, early, bulk)
+    velocity, latent_next = finish(
+        kept, other, shown, step_size, latent, passed
+    )
+    return next_stale, velocity, latent_next
 
 
 def solution(mesh):

time: 45.7 us -> 43.8 us (0.958)
  Pallas kernels: 25.6 us -> 20.1 us
  starting transfers between devices: 9.45 us -> 11.9 us
  local copies, waits for them, and re-layouts: 4.15 us -> 5.39 us
    pallas_call x2, Pallas kernels: 19.8 us -> 14.4 us  [the longest x1 13.7 us: attend(): pl.pallas_call(attend_kernel, grid=(slots,), out_shape=(jax.ShapeDtypeStr...]
    ppermute x0 -> x1, starting transfers between devices: none -> 2.42 us  [shards(): other = lax.ppermute(away, 'tp', [(i, i ^ 1) for i in members])]
    transpose x0 -> x1, local copies, waits for them, and re-layouts: none -> 1.53 us  [apart(): return jnp.transpose(kv[0], (0, 2, 1, 3))]
    ppermute x3, waiting for transfers between devices: 5.26 us -> 4.24 us  [from_behind(): return lax.ppermute(block, axis, route)]
    ppermute x0 -> x1, waiting for transfers between devices: none -> 0.74 us  [shards(): other = lax.ppermute(away, 'tp', [(i, i ^ 1) for i in members])]
    unnamed x26 -> x21, local copies, waits for them, and re-layouts: 4.06 us -> 3.75 us
  transfers between devices with their start and end apart: 3 -> 4, of which waited for: 1 -> 3; matrix products, arithmetic and copies ran while one was open for 1% -> 4% of each run, Pallas kernels for 50% -> 45%
where the time goes in v3:
time: 43.8 us; the launch traced here: 43.2 us
  Pallas kernels  20.1 us (46%)
  starting transfers between devices  11.9 us (27%)
  local copies, waits for them, and re-layouts  5.39 us (12%)
  waiting for transfers between devices  4.98 us (11%)
  between operations  0.82 us (2%)
    pallas_call x1, Pallas kernels, attend(): pl.pallas_call(attend_kernel, grid=(slots,), out_shape=(jax.ShapeDtypeStr...  13.7 us
    ppermute x3, starting transfers between devices, from_behind(): return lax.ppermute(block, axis, route)  9.46 us
    ppermute x3, waiting for transfers between devices, from_behind(): return lax.ppermute(block, axis, route)  4.24 us
    unnamed x21, local copies, waits for them, and re-layouts  3.75 us
    pallas_call x1, Pallas kernels, unpack(): pl.pallas_call(unpack_kernel, out_shape=(jax.ShapeDtypeStruct((1, slots,...  2.65 us
    ppermute x1, starting transfers between devices, shards(): other = lax.ppermute(away, 'tp', [(i, i ^ 1) for i in members])  2.42 us
    pallas_call x1, Pallas kernels, pack(): pl.pallas_call(pack_kernel, out_shape=(jax.ShapeDtypeStruct((1, slots, li...  2.19 us
    transpose x1, local copies, waits for them, and re-layouts, apart(): return jnp.transpose(kv[0], (0, 2, 1, 3))  1.53 us
  transfers between devices with their start and end apart: 4, of which 3 were waited for; matrix products, arithmetic and copies ran while one was open for 4% of the time, Pallas kernels for 45%

profile of v3, /device:TPU:6, one launch (start us, length us, event | category | flops | bytes accessed | tf_op | source)
XLA Modules:
  0.0 43.2 jit_solution(9254398424894981587)
XLA Ops:
  0.6 3.5 %collective-permute-start.2 = (bf16[1,2,256,2,256]{4,3,2,1,0:T(2,128)(2,1)}, bf16[1,2,256,2,256]{4,3,2,1,0:T(2,128)(2,1)S(1)}, u32[]{:S(2)}, u32[]{:S(2)}) collective-permute-start(bf16[1,2,256,2,256]{4,3,2,1,0:T(2,128)(2,1)} %param.13), channel_id=1, source_target_pairs={{256,0},{264,8},{272,16},{280,24},{288,32},{296,40},{304,48},{312,... | collective-permute-start | bytes 1572872 | tf_op jit(solution)/shard_map/ppermute | solution.py:26
  4.1 1.2 %copy-done = bf16[1,2,512,2,256]{4,3,2,1,0:T(2,128)(2,1)S(1)} copy-done((bf16[1,2,512,2,256]{4,3,2,1,0:T(2,128)(2,1)S(1)}, bf16[1,2,512,2,256]{4,3,2,1,0:T(2,128)(2,1)}, u32[]{:S(2)}) %copy-start) | copy-done | bytes 1048600
  5.4 0.8 %copy-done.2 = s32[64,2,64]{2,1,0:T(2,128)S(1)} copy-done((s32[64,2,64]{2,1,0:T(2,128)S(1)}, s32[64,2,64]{2,1,0:T(2,128)}, u32[]{:S(2)}) %copy-start.2) | copy-done | bytes 32792
  6.2 2.2 %pack.1 = (bf16[1,2,64,2,256]{4,3,2,1,0:T(2,128)(2,1)S(1)}, bf16[1,2,448,2,256]{4,3,2,1,0:T(2,128)(2,1)S(1)}) custom-call(s32[64,2,64]{2,1,0:T(2,128)S(1)} %copy-done.2, bf16[1,2,512,2,256]{4,3,2,1,0:T(2,128)(2,1)S(1)} %copy-done), custom_call_target="tpu_custom_call" | custom-call | bytes 4194304 | tf_op jit(solution)/shard_map/pack/pallas_call | solution.py:111
  8.4 2.4 %collective-permute-start = (bf16[1,2,64,2,256]{4,3,2,1,0:T(2,128)(2,1)S(1)}, bf16[1,2,64,2,256]{4,3,2,1,0:T(2,128)(2,1)S(1)}, u32[]{:S(2)}, u32[]{:S(2)}) collective-permute-start(bf16[1,2,64,2,256]{4,3,2,1,0:T(2,128)(2,1)S(1)} %get-tuple-element.22), channel_id=1, source_target_pairs={{256,0},{264,8},{272,16},{280,24},{288,32},{296,40},{304,48},{312,... | collective-permute-start | bytes 393224 | tf_op jit(solution)/shard_map/ppermute | solution.py:26
  10.8 0.0 copy-start.4
  10.8 0.0 copy-start.6
  10.8 0.6 %copy-done.4 = s32[64,2]{0,1:T(2,128)S(1)} copy-done((s32[64,2]{0,1:T(2,128)S(1)}, s32[64,2]{0,1:T(2,128)}, u32[]{:S(2)}) %copy-start.4) | copy-done | bytes 536
  11.4 0.8 %prepare.1 = (f32[2,1,1152]{2,1,0:T(1,128)S(1)}, s32[8,128]{1,0:T(8,128)S(1)}, f32[2,64,64]{2,1,0:T(8,128)S(1)}, f32[2,64,64]{2,1,0:T(8,128)S(1)}) custom-call(s32[64,2,64]{2,1,0:T(2,128)S(1)} %copy-done.2, s32[2,64]{1,0:T(2,128)S(1)} %bitcast.28, s32[64]{0:T(128)S(1)} %copy-done.6, s32[2,64]{1,0:T(2,128)S(1)} %bitcast.29), custom_call_target="tpu_custom_call" | custom-call | bytes 1048576 | tf_op jit(solution)/shard_map/prepare/pallas_call | solution.py:267
  12.3 0.0 copy-start.9
  12.3 3.6 %collective-permute-start.1 = (bf16[1,2,448,2,256]{4,3,2,1,0:T(2,128)(2,1)S(1)}, bf16[1,2,448,2,256]{4,3,2,1,0:T(2,128)(2,1)S(1)}, u32[]{:S(2)}, u32[]{:S(2)}) collective-permute-start(bf16[1,2,448,2,256]{4,3,2,1,0:T(2,128)(2,1)S(1)} %get-tuple-element.23), channel_id=1, source_target_pairs={{256,0},{264,8},{272,16},{280,24},{288,32},{296,40},{304,48},{312,... | collective-permute-start | bytes 2752520 | tf_op jit(solution)/shard_map/ppermute | solution.py:26
  15.9 1.5 %copy_bitcast_fusion = (bf16[2,2,512,256]{3,2,1,0:T(8,128)(2,1)S(1)}, bf16[2,2,512,256]{3,2,1,0:T(8,128)(2,1)S(1)}) fusion(bf16[1,2,512,2,256]{4,3,2,1,0:T(2,128)(2,1)} %param.12, bf16[1,2,512,2,256]{4,3,2,1,0:T(2,128)(2,1)S(1)} %copy-done.1), kind=kLoop, calls=%fused_computation | loop fusion | bytes 4194304 | tf_op jit(solution)/shard_map/transpose | solution.py:495
  17.5 0.1 copy.24
  17.6 2.8 %collective-permute-done.early = bf16[1,2,64,2,256]{4,3,2,1,0:T(2,128)(2,1)S(1)} collective-permute-done((bf16[1,2,64,2,256]{4,3,2,1,0:T(2,128)(2,1)S(1)}, bf16[1,2,64,2,256]{4,3,2,1,0:T(2,128)(2,1)S(1)}, u32[]{:S(2)}, u32[]{:S(2)}) %collective-permute-start) | collective-permute-done | bytes 131104 | tf_op jit(solution)/shard_map/ppermute | solution.py:26
  20.4 0.0 copy-start.7
  20.4 0.0 copy-start.8
  20.4 0.1 copy.23
  20.5 0.9 %copy-done.7 = bf16[1,2,512,256]{3,2,1,0:T(8,128)(2,1)S(1)} copy-done((bf16[1,2,512,256]{3,2,1,0:T(8,128)(2,1)S(1)}, bf16[1,2,512,256]{3,2,1,0:T(8,128)(2,1)}, u32[]{:S(2)}) %copy-start.7) | copy-done | bytes 524312
  21.5 13.7 %attend.1 = (f32[64,128]{1,0:T(8,128)S(1)}, bf16[64,128]{1,0:T(8,128)(2,1)S(1)}) custom-call(f32[2,1,1152]{2,1,0:T(1,128)S(1)} %get-tuple-element.25.bias, bf16[1,2,512,256]{3,2,1,0:T(8,128)(2,1)S(1)} %copy-done.7, bf16[2,2,512,256]{3,2,1,0:T(8,128)(2,1)S(1)} %get-tuple-element.34.own, bf16[2,2,512,256]{3,2,1,0:T(8,128)(2,1)S(1)} %get-tuple-element.33.stale, ...), custom_call_target="tpu_custom_call" | custom-call | flops 17448304640 | bytes 4194304 | tf_op jit(solution)/shard_map/attend/pallas_call | solution.py:452
  35.2 2.4 %collective-permute-start.3 = (bf16[64,128]{1,0:T(8,128)(2,1)S(1)}, bf16[64,128]{1,0:T(8,128)(2,1)S(1)}, u32[]{:S(2)}, u32[]{:S(2)}) collective-permute-start(bf16[64,128]{1,0:T(8,128)(2,1)S(1)} %get-tuple-element.27), channel_id=1, source_target_pairs={{0,1},{1,0},{2,3},{3,2},{4,5},{5,4},{6,7},{7,6},{8,9},{9,8},{10,11... | collective-permute-start | bytes 49160 | tf_op jit(solution)/shard_map/ppermute | solution.py:536
  37.6 1.4 %collective-permute-done.1.bulk = bf16[1,2,448,2,256]{4,3,2,1,0:T(2,128)(2,1)S(1)} collective-permute-done((bf16[1,2,448,2,256]{4,3,2,1,0:T(2,128)(2,1)S(1)}, bf16[1,2,448,2,256]{4,3,2,1,0:T(2,128)(2,1)S(1)}, u32[]{:S(2)}, u32[]{:S(2)}) %collective-permute-start.1) | collective-permute-done | bytes 917536 | tf_op jit(solution)/shard_map/ppermute | solution.py:26
  39.0 2.7 %unpack.1 = (bf16[1,2,512,2,256]{4,3,2,1,0:T(2,128)(2,1)}, f32[8,128]{1,0:T(8,128)S(1)}) custom-call(s32[8,128]{1,0:T(8,128)S(1)} %get-tuple-element.21.where, bf16[1,2,64,2,256]{4,3,2,1,0:T(2,128)(2,1)S(1)} %collective-permute-done.early, bf16[1,2,448,2,256]{4,3,2,1,0:T(2,128)(2,1)S(1)} %collective-permute-done.1.bulk), custom_call_target="tpu_custom_call" | custom-call | bytes 4194304 | tf_op jit(solution)/shard_map/unpack/pallas_call | solution.py:179
  41.7 0.7 %collective-permute-done.3.other = bf16[64,128]{1,0:T(8,128)(2,1)S(1)} collective-permute-done((bf16[64,128]{1,0:T(8,128)(2,1)S(1)}, bf16[64,128]{1,0:T(8,128)(2,1)S(1)}, u32[]{:S(2)}, u32[]{:S(2)}) %collective-permute-start.3) | collective-permute-done | bytes 16416 | tf_op jit(solution)/shard_map/ppermute | solution.py:536
  42.4 0.7 %finish.1 = (f32[1,2,64,64]{3,2,1,0:T(8,128)}, f32[1,2,64,64]{3,2,1,0:T(8,128)}) custom-call(f32[64,128]{1,0:T(8,128)S(1)} %get-tuple-element.26.kept, bf16[64,128]{1,0:T(8,128)(2,1)S(1)} %collective-permute-done.3.other, f32[2,64,64]{2,1,0:T(8,128)S(1)} %get-tuple-element.28.shown, f32[2,64,64]{2,1,0:T(8,128)S(1)} %get-tuple-element.29.step_size, ...), custom_call_target="tpu_custom_call" | custom-call | bytes 262144 | tf_op jit(solution)/shard_map/finish/pallas_call | solution.py:210
  (14 shorter events, 0.1 us)
Async XLA Ops:
  0.6 19.8 %collective-permute-start.2 = (bf16[1,2,256,2,256]{4,3,2,1,0:T(2,128)(2,1)}, bf16[1,2,256,2,256]{4,3,2,1,0:T(2,128)(2,1)S(1)}, u32[]{:S(2)}, u32[]{:S(2)}) collective-permute-start(bf16[1,2,256,2,256]{4,3,2,1,0:T(2,128)(2,1)} %param.13), channel_id=1, source_target_pairs={{256,0},{264,8},{272,16},{280,24},{288,32},{296,40},{304,48},{312,... | collective-permute-start | bytes 1572872 | tf_op jit(solution)/shard_map/ppermute | solution.py:26
  4.1 1.2 %copy-start = (bf16[1,2,512,2,256]{4,3,2,1,0:T(2,128)(2,1)S(1)}, bf16[1,2,512,2,256]{4,3,2,1,0:T(2,128)(2,1)}, u32[]{:S(2)}) copy-start(bf16[1,2,512,2,256]{4,3,2,1,0:T(2,128)(2,1)} %fresh.1) | copy-start | bytes 3145732
  5.4 0.8 %copy-start.2 = (s32[64,2,64]{2,1,0:T(2,128)S(1)}, s32[64,2,64]{2,1,0:T(2,128)}, u32[]{:S(2)}) copy-start(s32[64,2,64]{2,1,0:T(2,128)} %lists.3) | copy-start | bytes 98308
  6.2 4.6 %copy-start.5 = (s32[64,2]{0,1:T(2,128)S(1)}, s32[64,2]{0,1:T(2,128)}, u32[]{:S(2)}) copy-start(s32[64,2]{0,1:T(2,128)} %param.19) | copy-start | bytes 1540
  6.2 9.7 %copy-start.1 = (bf16[1,2,512,2,256]{4,3,2,1,0:T(2,128)(2,1)S(1)}, bf16[1,2,512,2,256]{4,3,2,1,0:T(2,128)(2,1)}, u32[]{:S(2)}) copy-start(bf16[1,2,512,2,256]{4,3,2,1,0:T(2,128)(2,1)} %fresh.1) | copy-start | bytes 3145732
  8.4 12.0 %collective-permute-start = (bf16[1,2,64,2,256]{4,3,2,1,0:T(2,128)(2,1)S(1)}, bf16[1,2,64,2,256]{4,3,2,1,0:T(2,128)(2,1)S(1)}, u32[]{:S(2)}, u32[]{:S(2)}) collective-permute-start(bf16[1,2,64,2,256]{4,3,2,1,0:T(2,128)(2,1)S(1)} %get-tuple-element.22), channel_id=1, source_target_pairs={{256,0},{264,8},{272,16},{280,24},{288,32},{296,40},{304,48},{312,... | collective-permute-start | bytes 393224 | tf_op jit(solution)/shard_map/ppermute | solution.py:26
  10.8 0.7 %copy-start.4 = (s32[64,2]{0,1:T(2,128)S(1)}, s32[64,2]{0,1:T(2,128)}, u32[]{:S(2)}) copy-start(s32[64,2]{0,1:T(2,128)} %param.16) | copy-start | bytes 1540
  10.8 0.7 %copy-start.6 = (s32[64]{0:T(128)S(1)}, s32[64]{0:T(128)}, u32[]{:S(2)}) copy-start(s32[64]{0:T(128)} %requests.1) | copy-start | bytes 772
  12.3 5.2 %copy-start.9 = (bf16[1,2,256,2,256]{4,3,2,1,0:T(2,128)(2,1)S(1)}, bf16[1,2,256,2,256]{4,3,2,1,0:T(2,128)(2,1)}, u32[]{:S(2)}) copy-start(bf16[1,2,256,2,256]{4,3,2,1,0:T(2,128)(2,1)} %param.13) | copy-start | bytes 1572868
  12.3 26.7 %collective-permute-start.1 = (bf16[1,2,448,2,256]{4,3,2,1,0:T(2,128)(2,1)S(1)}, bf16[1,2,448,2,256]{4,3,2,1,0:T(2,128)(2,1)S(1)}, u32[]{:S(2)}, u32[]{:S(2)}) collective-permute-start(bf16[1,2,448,2,256]{4,3,2,1,0:T(2,128)(2,1)S(1)} %get-tuple-element.23), channel_id=1, source_target_pairs={{256,0},{264,8},{272,16},{280,24},{288,32},{296,40},{304,48},{312,... | collective-permute-start | bytes 2752520 | tf_op jit(solution)/shard_map/ppermute | solution.py:26
  20.4 1.0 %copy-start.7 = (bf16[1,2,512,256]{3,2,1,0:T(8,128)(2,1)S(1)}, bf16[1,2,512,256]{3,2,1,0:T(8,128)(2,1)}, u32[]{:S(2)}) copy-start(bf16[1,2,512,256]{3,2,1,0:T(8,128)(2,1)} %q.1) | copy-start | bytes 1572868
  20.4 1.0 %copy-start.8 = (bf16[256,64]{0,1:T(8,128)(2,1)S(1)}, bf16[256,64]{0,1:T(8,128)(2,1)}, u32[]{:S(2)}) copy-start(bf16[256,64]{0,1:T(8,128)(2,1)} %param.14) | copy-start | bytes 98308
  35.2 7.3 %copy-start.3 = (f32[1,2,64,64]{3,2,1,0:T(8,128)S(1)}, f32[1,2,64,64]{3,2,1,0:T(8,128)}, u32[]{:S(2)}) copy-start(f32[1,2,64,64]{3,2,1,0:T(8,128)} %latent.1) | copy-start | bytes 98308
  35.2 7.3 %collective-permute-start.3 = (bf16[64,128]{1,0:T(8,128)(2,1)S(1)}, bf16[64,128]{1,0:T(8,128)(2,1)S(1)}, u32[]{:S(2)}, u32[]{:S(2)}) collective-permute-start(bf16[64,128]{1,0:T(8,128)(2,1)S(1)} %get-tuple-element.27), channel_id=1, source_target_pairs={{0,1},{1,0},{2,3},{3,2},{4,5},{5,4},{6,7},{7,6},{8,9},{9,8},{10,11... | collective-permute-start | bytes 49160 | tf_op jit(solution)/shard_map/ppermute | solution.py:536

commit v4 on v3

--- a/solution.py
+++ b/solution.py
@@ -221,8 +221,22 @@
 
 
 def prepare_kernel(
-    lists, live, requests, times, bias, where, shown, step, theirs, list_sem
+    lists,
+    live,
+    requests,
+    times,
+    queries,
+    bias,
+    where,
+    shown,
+    step,
+    queries_near,
+    theirs,
+    list_sem,
+    q_sem,
 ):
+    load_q = pltpu.make_async_copy(queries, queries_near, q_sem)
+    load_q.start()
     slots = bias.shape[0]
     listed = lists.shape[2]
     rows = (bias.shape[2] - TILE) // 2
@@ -259,9 +273,11 @@
         gap = times[1, request] - times[0, request]
         shown[s] = jnp.where(share_ids < live[s, group], 1.0, 0.0)
         step[s] = jnp.full((share, ch), gap, jnp.int32).astype(jnp.float32) / 1000.0
-
-
-def prepare(refresh_rows, live_t, request_list, times_t, rows, latent):
+    load_q.wait()
+
+
+def prepare(refresh_rows, live_t, request_list, times_t, queries, latent):
+    rows = queries.shape[2]
     _, slots, listed = refresh_rows.shape
     aside = jax.ShapeDtypeStruct(latent.shape[1:], jnp.float32)
     return pl.pallas_call(
@@ -271,11 +287,13 @@
             jax.ShapeDtypeStruct((8, TILE), jnp.int32),
             aside,
             aside,
-        ),
-        in_specs=[whole(HBM), whole(SMEM), whole(SMEM), whole(SMEM)],
-        out_specs=(whole(VMEM),) * 4,
+            jax.ShapeDtypeStruct(queries.shape, queries.dtype),
+        ),
+        in_specs=[whole(HBM), whole(SMEM), whole(SMEM), whole(SMEM), whole(HBM)],
+        out_specs=(whole(VMEM),) * 5,
         scratch_shapes=[
             pltpu.VMEM((slots, listed), jnp.int32),
+            pltpu.SemaphoreType.DMA,
             pltpu.SemaphoreType.DMA,
         ],
         compiler_params=pltpu.CompilerParams(vmem_limit_bytes=4 << 20),
@@ -283,7 +301,7 @@
             flops=0, transcendentals=0, bytes_accessed=1 << 20
         ),
         name="prepare",
-    )(refresh_rows, live_t, request_list, times_t)
+    )(refresh_rows, live_t, request_list, times_t, queries)
 
 
 def tiles(array):
@@ -510,23 +528,25 @@
     half_groups = lax.axis_size("grp") // 2
     live_t = live_counts.T
     times_t = timesteps.T
-    rows = fresh_kv.shape[2]
     listed = refresh_rows.shape[2]
     text_other = in_order(from_behind(in_order(text_kv), "grp", half_groups))
     early_out, bulk_out = pack(refresh_rows, fresh_kv)
     early = in_order(from_behind(in_order(early_out), "grp", half_groups))
-    bias, where, shown, step_size = prepare(
-        refresh_rows, live_t, request_list, times_t, rows, latent
-    )
-    bulk_out, bias, where = lax.optimization_barrier((bulk_out, bias, where))
+    bias, where, shown, step_size, near = prepare(
+        refresh_rows, live_t, request_list, times_t, queries, latent
+    )
+    own, stale, text = apart(fresh_kv), apart(stale_kv), apart(text_kv)
+    bulk_out, bias, where, near, own, stale, text = lax.optimization_barrier(
+        (bulk_out, bias, where, near, own, stale, text)
+    )
     bulk = from_behind(bulk_out, "grp", half_groups)
     early_apart = jnp.pad(apart(early), ((0, 0), (0, 0), (0, TILE - listed), (0, 0)))
     kept, away = attend(
         bias,
-        queries,
-        apart(fresh_kv),
-        apart(stale_kv),
-        apart(text_kv),
+        near,
+        own,
+        stale,
+        text,
         apart(text_other),
         early_apart,
         w_velocity.T,

time: 43.8 us -> 43.3 us (0.989)
  waiting for transfers between devices: 4.98 us -> 3.53 us
  local copies, waits for them, and re-layouts: 5.39 us -> 6.2 us
  Pallas kernels: 20.1 us -> 19.3 us
  starting transfers between devices: 11.9 us -> 12.6 us
    unnamed x21 -> x25, local copies, waits for them, and re-layouts: 3.75 us -> 6.09 us
    transpose x1 -> x0, local copies, waits for them, and re-layouts: 1.53 us -> none  [apart(): return jnp.transpose(kv[0], (0, 2, 1, 3))]
    ppermute x1, starting transfers between devices: 2.42 us -> 3.3 us  [shards(): other = lax.ppermute(away, 'tp', [(i, i ^ 1) for i in members])]
    pallas_call x1, Pallas kernels: 13.7 us -> 12.8 us  [attend(): pl.pallas_call(attend_kernel, grid=(slots,), out_shape=(jax.ShapeDtypeStr...]
    ppermute x1, waiting for transfers between devices: 0.74 us -> 0.01 us  [shards(): other = lax.ppermute(away, 'tp', [(i, i ^ 1) for i in members])]
    ppermute x3, waiting for transfers between devices: 4.24 us -> 3.53 us  [from_behind(): return lax.ppermute(block, axis, route)]
  transfers between devices with their start and end apart: 4 -> 4, of which waited for: 3 -> 2; matrix products, arithmetic and copies ran while one was open for 4% -> 4% of each run, Pallas kernels for 45% -> 44%
where the time goes in v4:
time: 43.3 us; the launch traced here: 42.5 us
  Pallas kernels  19.3 us (45%)
  starting transfers between devices  12.6 us (29%)
  local copies, waits for them, and re-layouts  6.2 us (14%)
  waiting for transfers between devices  3.53 us (8%)
  between operations  0.82 us (2%)
    pallas_call x1, Pallas kernels, attend(): pl.pallas_call(attend_kernel, grid=(slots,), out_shape=(jax.ShapeDtypeStr...  12.8 us
    ppermute x3, starting transfers between devices, from_behind(): return lax.ppermute(block, axis, route)  9.33 us
    unnamed x25, local copies, waits for them, and re-layouts  6.09 us
    ppermute x3, waiting for transfers between devices, from_behind(): return lax.ppermute(block, axis, route)  3.53 us
    ppermute x1, starting transfers between devices, shards(): other = lax.ppermute(away, 'tp', [(i, i ^ 1) for i in members])  3.3 us
    pallas_call x1, Pallas kernels, unpack(): pl.pallas_call(unpack_kernel, out_shape=(jax.ShapeDtypeStruct((1, slots,...  2.65 us
    pallas_call x1, Pallas kernels, pack(): pl.pallas_call(pack_kernel, out_shape=(jax.ShapeDtypeStruct((1, slots, li...  2.19 us
    pallas_call x1, Pallas kernels, prepare(): pl.pallas_call(prepare_kernel, out_shape=(jax.ShapeDtypeStruct((slots, 1,...  0.89 us
  transfers between devices with their start and end apart: 4, of which 2 were waited for; matrix products, arithmetic and copies ran while one was open for 4% of the time, Pallas kernels for 44%

profile of v4, /device:TPU:6, one launch (start us, length us, event | category | flops | bytes accessed | tf_op | source)
XLA Modules:
  0.0 42.5 jit_solution(1740555049022429668)
XLA Ops:
  0.6 3.5 %collective-permute-start.2 = (bf16[1,2,256,2,256]{4,3,2,1,0:T(2,128)(2,1)}, bf16[1,2,256,2,256]{4,3,2,1,0:T(2,128)(2,1)S(1)}, u32[]{:S(2)}, u32[]{:S(2)}) collective-permute-start(bf16[1,2,256,2,256]{4,3,2,1,0:T(2,128)(2,1)} %param.13), channel_id=1, source_target_pairs={{256,0},{264,8},{272,16},{280,24},{288,32},{296,40},{304,48},{312,... | collective-permute-start | bytes 1572872 | tf_op jit(solution)/shard_map/ppermute | solution.py:26
  4.1 1.2 %copy-done = bf16[1,2,512,2,256]{4,3,2,1,0:T(2,128)(2,1)S(1)} copy-done((bf16[1,2,512,2,256]{4,3,2,1,0:T(2,128)(2,1)S(1)}, bf16[1,2,512,2,256]{4,3,2,1,0:T(2,128)(2,1)}, u32[]{:S(2)}) %copy-start) | copy-done | bytes 1048600
  5.4 0.8 %copy-done.3 = s32[64,2,64]{2,1,0:T(2,128)S(1)} copy-done((s32[64,2,64]{2,1,0:T(2,128)S(1)}, s32[64,2,64]{2,1,0:T(2,128)}, u32[]{:S(2)}) %copy-start.3) | copy-done | bytes 32792
  6.2 2.2 %pack.1 = (bf16[1,2,64,2,256]{4,3,2,1,0:T(2,128)(2,1)S(1)}, bf16[1,2,448,2,256]{4,3,2,1,0:T(2,128)(2,1)S(1)}) custom-call(s32[64,2,64]{2,1,0:T(2,128)S(1)} %copy-done.3, bf16[1,2,512,2,256]{4,3,2,1,0:T(2,128)(2,1)S(1)} %copy-done), custom_call_target="tpu_custom_call" | custom-call | bytes 4194304 | tf_op jit(solution)/shard_map/pack/pallas_call | solution.py:111
  8.4 2.4 %collective-permute-start = (bf16[1,2,64,2,256]{4,3,2,1,0:T(2,128)(2,1)S(1)}, bf16[1,2,64,2,256]{4,3,2,1,0:T(2,128)(2,1)S(1)}, u32[]{:S(2)}, u32[]{:S(2)}) collective-permute-start(bf16[1,2,64,2,256]{4,3,2,1,0:T(2,128)(2,1)S(1)} %get-tuple-element.28), channel_id=1, source_target_pairs={{256,0},{264,8},{272,16},{280,24},{288,32},{296,40},{304,48},{312,... | collective-permute-start | bytes 393224 | tf_op jit(solution)/shard_map/ppermute | solution.py:26
  10.8 1.1 %copy.26 = bf16[1,2,256,2,256]{4,2,3,1,0:T(8,128)(2,1)S(1)} copy(bf16[1,2,256,2,256]{4,3,2,1,0:T(2,128)(2,1)} %param.13) | data formatting | bytes 1048576 | tf_op args[3]
  11.9 0.0 copy-start.10
  11.9 0.1 copy.24
  12.0 1.1 %copy-done.10 = bf16[1,2,512,2,256]{4,3,2,1,0:T(2,128)(2,1)S(1)} copy-done((bf16[1,2,512,2,256]{4,3,2,1,0:T(2,128)(2,1)S(1)}, bf16[1,2,512,2,256]{4,3,2,1,0:T(2,128)(2,1)}, u32[]{:S(2)}) %copy-start.10) | copy-done | bytes 1048600
  13.1 0.1 copy.23
  13.3 0.0 copy-start.6
  13.3 0.0 copy-start.8
  13.3 0.9 %copy-done.2 = bf16[1,2,512,256]{3,2,1,0:T(8,128)(2,1)S(1)} copy-done((bf16[1,2,512,256]{3,2,1,0:T(8,128)(2,1)S(1)}, bf16[1,2,512,256]{3,2,1,0:T(8,128)(2,1)}, u32[]{:S(2)}) %copy-start.2) | copy-done | bytes 524312
  14.2 0.9 %prepare.1 = (f32[2,1,1152]{2,1,0:T(1,128)S(1)}, s32[8,128]{1,0:T(8,128)S(1)}, f32[2,64,64]{2,1,0:T(8,128)S(1)}, f32[2,64,64]{2,1,0:T(8,128)S(1)}, bf16[1,2,512,256]{3,2,1,0:T(8,128)(2,1)S(1)}) custom-call(s32[64,2,64]{2,1,0:T(2,128)S(1)} %copy-done.4, s32[2,64]{1,0:T(2,128)S(1)} %bitcast.32, s32[64]{0:T(128)S(1)} %copy-done.8, s32[2,64]{1,0:T(2,128)S(1)} %bitcast.33, ...), custom_call_target="tpu_custom_call" | custom-call | bytes 1048576 | tf_op jit(solution)/shard_map/prepare/pallas_call | solution.py:283
  15.1 3.5 %collective-permute-start.1 = (bf16[1,2,448,2,256]{4,3,2,1,0:T(2,128)(2,1)S(1)}, bf16[1,2,448,2,256]{4,3,2,1,0:T(2,128)(2,1)S(1)}, u32[]{:S(2)}, u32[]{:S(2)}) collective-permute-start(bf16[1,2,448,2,256]{4,3,2,1,0:T(2,128)(2,1)S(1)} %get-tuple-element.29), channel_id=1, source_target_pairs={{256,0},{264,8},{272,16},{280,24},{288,32},{296,40},{304,48},{312,... | collective-permute-start | bytes 2752520 | tf_op jit(solution)/shard_map/ppermute | solution.py:26
  18.6 1.0 %collective-permute-done.early = bf16[1,2,64,2,256]{4,3,2,1,0:T(2,128)(2,1)S(1)} collective-permute-done((bf16[1,2,64,2,256]{4,3,2,1,0:T(2,128)(2,1)S(1)}, bf16[1,2,64,2,256]{4,3,2,1,0:T(2,128)(2,1)S(1)}, u32[]{:S(2)}, u32[]{:S(2)}) %collective-permute-start) | collective-permute-done | bytes 131104 | tf_op jit(solution)/shard_map/ppermute | solution.py:26
  19.6 0.1 copy.25
  19.7 0.7 %copy-done.9 = bf16[256,64]{0,1:T(8,128)(2,1)S(1)} copy-done((bf16[256,64]{0,1:T(8,128)(2,1)S(1)}, bf16[256,64]{0,1:T(8,128)(2,1)}, u32[]{:S(2)}) %copy-start.9) | copy-done | bytes 32792
  20.3 12.8 %attend.1 = (f32[64,128]{1,0:T(8,128)S(1)}, bf16[64,128]{1,0:T(8,128)(2,1)S(1)}) custom-call(f32[2,1,1152]{2,1,0:T(1,128)S(1)} %get-tuple-element.31.bias, bf16[1,2,512,256]{3,2,1,0:T(8,128)(2,1)S(1)} %get-tuple-element.32.q, bf16[2,2,512,256]{3,2,1,0:T(8,128)(2,1)S(1)} %bitcast.28, bf16[2,2,512,256]{3,2,1,0:T(8,128)(2,1)S(1)} %bitcast.29, ...), custom_call_target="tpu_custom_call" | custom-call | flops 17448304640 | bytes 4194304 | tf_op jit(solution)/shard_map/attend/pallas_call | solution.py:470
  33.2 0.0 copy-start.5
  33.2 3.3 %collective-permute-start.3 = (bf16[64,128]{1,0:T(8,128)(2,1)S(1)}, bf16[64,128]{1,0:T(8,128)(2,1)S(1)}, u32[]{:S(2)}, u32[]{:S(2)}) collective-permute-start(bf16[64,128]{1,0:T(8,128)(2,1)S(1)} %get-tuple-element.37), channel_id=1, source_target_pairs={{0,1},{1,0},{2,3},{3,2},{4,5},{5,4},{6,7},{7,6},{8,9},{9,8},{10,11... | collective-permute-start | bytes 49160 | tf_op jit(solution)/shard_map/ppermute | solution.py:556
  36.5 2.6 %collective-permute-done.1.bulk = bf16[1,2,448,2,256]{4,3,2,1,0:T(2,128)(2,1)S(1)} collective-permute-done((bf16[1,2,448,2,256]{4,3,2,1,0:T(2,128)(2,1)S(1)}, bf16[1,2,448,2,256]{4,3,2,1,0:T(2,128)(2,1)S(1)}, u32[]{:S(2)}, u32[]{:S(2)}) %collective-permute-start.1) | collective-permute-done | bytes 917536 | tf_op jit(solution)/shard_map/ppermute | solution.py:26
  39.0 2.7 %unpack.1 = (bf16[1,2,512,2,256]{4,3,2,1,0:T(2,128)(2,1)}, f32[8,128]{1,0:T(8,128)S(1)}) custom-call(s32[8,128]{1,0:T(8,128)S(1)} %get-tuple-element.27.where, bf16[1,2,64,2,256]{4,3,2,1,0:T(2,128)(2,1)S(1)} %collective-permute-done.early, bf16[1,2,448,2,256]{4,3,2,1,0:T(2,128)(2,1)S(1)} %collective-permute-done.1.bulk), custom_call_target="tpu_custom_call" | custom-call | bytes 4194304 | tf_op jit(solution)/shard_map/unpack/pallas_call | solution.py:179
  41.7 0.7 %finish.1 = (f32[1,2,64,64]{3,2,1,0:T(8,128)}, f32[1,2,64,64]{3,2,1,0:T(8,128)}) custom-call(f32[64,128]{1,0:T(8,128)S(1)} %get-tuple-element.36.kept, bf16[64,128]{1,0:T(8,128)(2,1)S(1)} %collective-permute-done.3.other, f32[2,64,64]{2,1,0:T(8,128)S(1)} %get-tuple-element.38.shown, f32[2,64,64]{2,1,0:T(8,128)S(1)} %get-tuple-element.39.step_size, ...), custom_call_target="tpu_custom_call" | custom-call | bytes 262144 | tf_op jit(solution)/shard_map/finish/pallas_call | solution.py:210
  (17 shorter events, 0.1 us)
Async XLA Ops:
  0.6 19.0 %collective-permute-start.2 = (bf16[1,2,256,2,256]{4,3,2,1,0:T(2,128)(2,1)}, bf16[1,2,256,2,256]{4,3,2,1,0:T(2,128)(2,1)S(1)}, u32[]{:S(2)}, u32[]{:S(2)}) collective-permute-start(bf16[1,2,256,2,256]{4,3,2,1,0:T(2,128)(2,1)} %param.13), channel_id=1, source_target_pairs={{256,0},{264,8},{272,16},{280,24},{288,32},{296,40},{304,48},{312,... | collective-permute-start | bytes 1572872 | tf_op jit(solution)/shard_map/ppermute | solution.py:26
  4.1 1.2 %copy-start = (bf16[1,2,512,2,256]{4,3,2,1,0:T(2,128)(2,1)S(1)}, bf16[1,2,512,2,256]{4,3,2,1,0:T(2,128)(2,1)}, u32[]{:S(2)}) copy-start(bf16[1,2,512,2,256]{4,3,2,1,0:T(2,128)(2,1)} %fresh.1) | copy-start | bytes 3145732
  5.4 0.8 %copy-start.3 = (s32[64,2,64]{2,1,0:T(2,128)S(1)}, s32[64,2,64]{2,1,0:T(2,128)}, u32[]{:S(2)}) copy-start(s32[64,2,64]{2,1,0:T(2,128)} %lists.3) | copy-start | bytes 98308
  6.2 5.7 %copy-start.1 = (bf16[1,2,512,2,256]{4,3,2,1,0:T(2,128)(2,1)S(1)}, bf16[1,2,512,2,256]{4,3,2,1,0:T(2,128)(2,1)}, u32[]{:S(2)}) copy-start(bf16[1,2,512,2,256]{4,3,2,1,0:T(2,128)(2,1)} %fresh.1) | copy-start | bytes 3145732
  8.4 11.1 %collective-permute-start = (bf16[1,2,64,2,256]{4,3,2,1,0:T(2,128)(2,1)S(1)}, bf16[1,2,64,2,256]{4,3,2,1,0:T(2,128)(2,1)S(1)}, u32[]{:S(2)}, u32[]{:S(2)}) collective-permute-start(bf16[1,2,64,2,256]{4,3,2,1,0:T(2,128)(2,1)S(1)} %get-tuple-element.28), channel_id=1, source_target_pairs={{256,0},{264,8},{272,16},{280,24},{288,32},{296,40},{304,48},{312,... | collective-permute-start | bytes 393224 | tf_op jit(solution)/shard_map/ppermute | solution.py:26
  11.9 1.2 %copy-start.10 = (bf16[1,2,512,2,256]{4,3,2,1,0:T(2,128)(2,1)S(1)}, bf16[1,2,512,2,256]{4,3,2,1,0:T(2,128)(2,1)}, u32[]{:S(2)}) copy-start(bf16[1,2,512,2,256]{4,3,2,1,0:T(2,128)(2,1)} %param.12) | copy-start | bytes 3145732
  13.1 1.0 %copy-start.2 = (bf16[1,2,512,256]{3,2,1,0:T(8,128)(2,1)S(1)}, bf16[1,2,512,256]{3,2,1,0:T(8,128)(2,1)}, u32[]{:S(2)}) copy-start(bf16[1,2,512,256]{3,2,1,0:T(8,128)(2,1)} %queries.1) | copy-start | bytes 1572868
  13.1 1.0 %copy-start.4 = (s32[64,2,64]{2,1,0:T(2,128)S(1)}, s32[64,2,64]{2,1,0:T(2,128)}, u32[]{:S(2)}) copy-start(s32[64,2,64]{2,1,0:T(2,128)} %lists.3) | copy-start | bytes 98308
  13.1 1.0 %copy-start.7 = (s32[64,2]{0,1:T(2,128)S(1)}, s32[64,2]{0,1:T(2,128)}, u32[]{:S(2)}) copy-start(s32[64,2]{0,1:T(2,128)} %param.19) | copy-start | bytes 1540
  13.3 0.9 %copy-start.6 = (s32[64,2]{0,1:T(2,128)S(1)}, s32[64,2]{0,1:T(2,128)}, u32[]{:S(2)}) copy-start(s32[64,2]{0,1:T(2,128)} %param.16) | copy-start | bytes 1540
  13.3 0.9 %copy-start.8 = (s32[64]{0:T(128)S(1)}, s32[64]{0:T(128)}, u32[]{:S(2)}) copy-start(s32[64]{0:T(128)} %requests.1) | copy-start | bytes 772
  15.1 24.0 %collective-permute-start.1 = (bf16[1,2,448,2,256]{4,3,2,1,0:T(2,128)(2,1)S(1)}, bf16[1,2,448,2,256]{4,3,2,1,0:T(2,128)(2,1)S(1)}, u32[]{:S(2)}, u32[]{:S(2)}) collective-permute-start(bf16[1,2,448,2,256]{4,3,2,1,0:T(2,128)(2,1)S(1)} %get-tuple-element.29), channel_id=1, source_target_pairs={{256,0},{264,8},{272,16},{280,24},{288,32},{296,40},{304,48},{312,... | collective-permute-start | bytes 2752520 | tf_op jit(solution)/shard_map/ppermute | solution.py:26
  19.6 0.8 %copy-start.9 = (bf16[256,64]{0,1:T(8,128)(2,1)S(1)}, bf16[256,64]{0,1:T(8,128)(2,1)}, u32[]{:S(2)}) copy-start(bf16[256,64]{0,1:T(8,128)(2,1)} %param.14) | copy-start | bytes 98308
  33.2 8.6 %copy-start.5 = (f32[1,2,64,64]{3,2,1,0:T(8,128)S(1)}, f32[1,2,64,64]{3,2,1,0:T(8,128)}, u32[]{:S(2)}) copy-start(f32[1,2,64,64]{3,2,1,0:T(8,128)} %latent.1) | copy-start | bytes 98308
  33.2 8.5 %collective-permute-start.3 = (bf16[64,128]{1,0:T(8,128)(2,1)S(1)}, bf16[64,128]{1,0:T(8,128)(2,1)S(1)}, u32[]{:S(2)}, u32[]{:S(2)}) collective-permute-start(bf16[64,128]{1,0:T(8,128)(2,1)S(1)} %get-tuple-element.37), channel_id=1, source_target_pairs={{0,1},{1,0},{2,3},{3,2},{4,5},{5,4},{6,7},{7,6},{8,9},{9,8},{10,11... | collective-permute-start | bytes 49160 | tf_op jit(solution)/shard_map/ppermute | solution.py:556

commit v5 on v4

--- a/solution.py
+++ b/solution.py
@@ -134,8 +134,11 @@
     )(refresh_rows, fresh_kv)
 
 
-def unpack_kernel(where, early, bulk, out, passed, held, in_sem, out_sem):
-    passed[...] = jnp.zeros_like(passed)
+def unpack_kernel(
+    plan, early, bulk, out, passed, held, where, plan_sem, in_sem, out_sem
+):
+    move = pltpu.make_async_copy(plan, where, plan_sem)
+    move.start()
     _, slots, rows, _, _ = out.shape
     listed = early.shape[2]
     keep = rows - listed
@@ -148,6 +151,8 @@
     ]
     for load in loads:
         load.start()
+    passed[...] = jnp.zeros_like(passed)
+    move.wait()
     stores = []
     for s in range(slots):
         loads[s].wait()
@@ -182,10 +187,12 @@
             jax.ShapeDtypeStruct((1, slots, rows, two, width), kv),
             jax.ShapeDtypeStruct((8, TILE), jnp.float32),
         ),
-        in_specs=[whole(SMEM), whole(VMEM), whole(pl.ANY)],
+        in_specs=[whole(VMEM), whole(VMEM), whole(pl.ANY)],
         out_specs=(whole(pl.ANY), whole(VMEM)),
         scratch_shapes=[
             pltpu.VMEM((slots, rows, two, width), kv),
+            pltpu.SMEM(where.shape, where.dtype),
+            pltpu.SemaphoreType.DMA,
             pltpu.SemaphoreType.DMA((slots,)),
             pltpu.SemaphoreType.DMA((slots,)),
         ],

time: 43.3 us -> 42.9 us (level)
  waiting for transfers between devices: 3.53 us -> 4.03 us
  Pallas kernels: 19.3 us -> 18.8 us
    pallas_call x1, Pallas kernels: 2.65 us -> 2.12 us  [unpack(): pl.pallas_call(unpack_kernel, out_shape=(jax.ShapeDtypeStruct((1, slots,...]
    ppermute x1, waiting for transfers between devices: 0.01 us -> 0.5 us  [shards(): other = lax.ppermute(away, 'tp', [(i, i ^ 1) for i in members])]
  transfers between devices with their start and end apart: 4 -> 4, of which waited for: 2 -> 3; matrix products, arithmetic and copies ran while one was open for 4% -> 4% of each run, Pallas kernels for 44% -> 43%
where the time goes in v5:
time: 42.9 us; the launch traced here: 42.4 us
  Pallas kernels  18.8 us (44%)
  starting transfers between devices  12.6 us (29%)
  local copies, waits for them, and re-layouts  6.2 us (14%)
  waiting for transfers between devices  4.03 us (9%)
  between operations  0.8 us (2%)
    pallas_call x1, Pallas kernels, attend(): pl.pallas_call(attend_kernel, grid=(slots,), out_shape=(jax.ShapeDtypeStr...  12.8 us
    ppermute x3, starting transfers between devices, from_behind(): return lax.ppermute(block, axis, route)  9.33 us
    unnamed x25, local copies, waits for them, and re-layouts  6.09 us
    ppermute x3, waiting for transfers between devices, from_behind(): return lax.ppermute(block, axis, route)  3.53 us
    ppermute x1, starting transfers between devices, shards(): other = lax.ppermute(away, 'tp', [(i, i ^ 1) for i in members])  3.3 us
    pallas_call x1, Pallas kernels, pack(): pl.pallas_call(pack_kernel, out_shape=(jax.ShapeDtypeStruct((1, slots, li...  2.19 us
    pallas_call x1, Pallas kernels, unpack(): pl.pallas_call(unpack_kernel, out_shape=(jax.ShapeDtypeStruct((1, slots,...  2.12 us
    pallas_call x1, Pallas kernels, prepare(): pl.pallas_call(prepare_kernel, out_shape=(jax.ShapeDtypeStruct((slots, 1,...  0.89 us
  transfers between devices with their start and end apart: 4, of which 3 were waited for; matrix products, arithmetic and copies ran while one was open for 4% of the time, Pallas kernels for 43%

profile of v5, /device:TPU:6, one launch (start us, length us, event | category | flops | bytes accessed | tf_op | source)
XLA Modules:
  0.0 42.4 jit_solution(15245649588050953341)
XLA Ops:
  0.6 3.5 %collective-permute-start.2 = (bf16[1,2,256,2,256]{4,3,2,1,0:T(2,128)(2,1)}, bf16[1,2,256,2,256]{4,3,2,1,0:T(2,128)(2,1)S(1)}, u32[]{:S(2)}, u32[]{:S(2)}) collective-permute-start(bf16[1,2,256,2,256]{4,3,2,1,0:T(2,128)(2,1)} %param.13), channel_id=1, source_target_pairs={{256,0},{264,8},{272,16},{280,24},{288,32},{296,40},{304,48},{312,... | collective-permute-start | bytes 1572872 | tf_op jit(solution)/shard_map/ppermute | solution.py:26
  4.1 1.2 %copy-done = bf16[1,2,512,2,256]{4,3,2,1,0:T(2,128)(2,1)S(1)} copy-done((bf16[1,2,512,2,256]{4,3,2,1,0:T(2,128)(2,1)S(1)}, bf16[1,2,512,2,256]{4,3,2,1,0:T(2,128)(2,1)}, u32[]{:S(2)}) %copy-start) | copy-done | bytes 1048600
  5.4 0.8 %copy-done.3 = s32[64,2,64]{2,1,0:T(2,128)S(1)} copy-done((s32[64,2,64]{2,1,0:T(2,128)S(1)}, s32[64,2,64]{2,1,0:T(2,128)}, u32[]{:S(2)}) %copy-start.3) | copy-done | bytes 32792
  6.2 2.2 %pack.1 = (bf16[1,2,64,2,256]{4,3,2,1,0:T(2,128)(2,1)S(1)}, bf16[1,2,448,2,256]{4,3,2,1,0:T(2,128)(2,1)S(1)}) custom-call(s32[64,2,64]{2,1,0:T(2,128)S(1)} %copy-done.3, bf16[1,2,512,2,256]{4,3,2,1,0:T(2,128)(2,1)S(1)} %copy-done), custom_call_target="tpu_custom_call" | custom-call | bytes 4194304 | tf_op jit(solution)/shard_map/pack/pallas_call | solution.py:111
  8.4 2.4 %collective-permute-start = (bf16[1,2,64,2,256]{4,3,2,1,0:T(2,128)(2,1)S(1)}, bf16[1,2,64,2,256]{4,3,2,1,0:T(2,128)(2,1)S(1)}, u32[]{:S(2)}, u32[]{:S(2)}) collective-permute-start(bf16[1,2,64,2,256]{4,3,2,1,0:T(2,128)(2,1)S(1)} %get-tuple-element.28), channel_id=1, source_target_pairs={{256,0},{264,8},{272,16},{280,24},{288,32},{296,40},{304,48},{312,... | collective-permute-start | bytes 393224 | tf_op jit(solution)/shard_map/ppermute | solution.py:26
  10.8 1.1 %copy.26 = bf16[1,2,256,2,256]{4,2,3,1,0:T(8,128)(2,1)S(1)} copy(bf16[1,2,256,2,256]{4,3,2,1,0:T(2,128)(2,1)} %param.13) | data formatting | bytes 1048576 | tf_op args[3]
  11.9 0.1 copy.24
  12.0 1.1 %copy-done.10 = bf16[1,2,512,2,256]{4,3,2,1,0:T(2,128)(2,1)S(1)} copy-done((bf16[1,2,512,2,256]{4,3,2,1,0:T(2,128)(2,1)S(1)}, bf16[1,2,512,2,256]{4,3,2,1,0:T(2,128)(2,1)}, u32[]{:S(2)}) %copy-start.10) | copy-done | bytes 1048600
  13.1 0.1 copy.23
  13.3 0.0 copy-start.6
  13.3 0.0 copy-start.8
  13.3 0.9 %copy-done.2 = bf16[1,2,512,256]{3,2,1,0:T(8,128)(2,1)S(1)} copy-done((bf16[1,2,512,256]{3,2,1,0:T(8,128)(2,1)S(1)}, bf16[1,2,512,256]{3,2,1,0:T(8,128)(2,1)}, u32[]{:S(2)}) %copy-start.2) | copy-done | bytes 524312
  14.2 0.9 %prepare.1 = (f32[2,1,1152]{2,1,0:T(1,128)S(1)}, s32[8,128]{1,0:T(8,128)S(1)}, f32[2,64,64]{2,1,0:T(8,128)S(1)}, f32[2,64,64]{2,1,0:T(8,128)S(1)}, bf16[1,2,512,256]{3,2,1,0:T(8,128)(2,1)S(1)}) custom-call(s32[64,2,64]{2,1,0:T(2,128)S(1)} %copy-done.4, s32[2,64]{1,0:T(2,128)S(1)} %bitcast.32, s32[64]{0:T(128)S(1)} %copy-done.8, s32[2,64]{1,0:T(2,128)S(1)} %bitcast.33, ...), custom_call_target="tpu_custom_call" | custom-call | bytes 1048576 | tf_op jit(solution)/shard_map/prepare/pallas_call | solution.py:290
  15.1 3.5 %collective-permute-start.1 = (bf16[1,2,448,2,256]{4,3,2,1,0:T(2,128)(2,1)S(1)}, bf16[1,2,448,2,256]{4,3,2,1,0:T(2,128)(2,1)S(1)}, u32[]{:S(2)}, u32[]{:S(2)}) collective-permute-start(bf16[1,2,448,2,256]{4,3,2,1,0:T(2,128)(2,1)S(1)} %get-tuple-element.29), channel_id=1, source_target_pairs={{256,0},{264,8},{272,16},{280,24},{288,32},{296,40},{304,48},{312,... | collective-permute-start | bytes 2752520 | tf_op jit(solution)/shard_map/ppermute | solution.py:26
  18.6 1.0 %collective-permute-done.early = bf16[1,2,64,2,256]{4,3,2,1,0:T(2,128)(2,1)S(1)} collective-permute-done((bf16[1,2,64,2,256]{4,3,2,1,0:T(2,128)(2,1)S(1)}, bf16[1,2,64,2,256]{4,3,2,1,0:T(2,128)(2,1)S(1)}, u32[]{:S(2)}, u32[]{:S(2)}) %collective-permute-start) | collective-permute-done | bytes 131104 | tf_op jit(solution)/shard_map/ppermute | solution.py:26
  19.6 0.1 copy.25
  19.7 0.7 %copy-done.9 = bf16[256,64]{0,1:T(8,128)(2,1)S(1)} copy-done((bf16[256,64]{0,1:T(8,128)(2,1)S(1)}, bf16[256,64]{0,1:T(8,128)(2,1)}, u32[]{:S(2)}) %copy-start.9) | copy-done | bytes 32792
  20.3 12.8 %attend.1 = (f32[64,128]{1,0:T(8,128)S(1)}, bf16[64,128]{1,0:T(8,128)(2,1)S(1)}) custom-call(f32[2,1,1152]{2,1,0:T(1,128)S(1)} %get-tuple-element.31.bias, bf16[1,2,512,256]{3,2,1,0:T(8,128)(2,1)S(1)} %get-tuple-element.32.q, bf16[2,2,512,256]{3,2,1,0:T(8,128)(2,1)S(1)} %bitcast.28, bf16[2,2,512,256]{3,2,1,0:T(8,128)(2,1)S(1)} %bitcast.29, ...), custom_call_target="tpu_custom_call" | custom-call | flops 17448304640 | bytes 4194304 | tf_op jit(solution)/shard_map/attend/pallas_call | solution.py:477
  33.2 0.0 copy-start.5
  33.2 3.3 %collective-permute-start.3 = (bf16[64,128]{1,0:T(8,128)(2,1)S(1)}, bf16[64,128]{1,0:T(8,128)(2,1)S(1)}, u32[]{:S(2)}, u32[]{:S(2)}) collective-permute-start(bf16[64,128]{1,0:T(8,128)(2,1)S(1)} %get-tuple-element.37), channel_id=1, source_target_pairs={{0,1},{1,0},{2,3},{3,2},{4,5},{5,4},{6,7},{7,6},{8,9},{9,8},{10,11... | collective-permute-start | bytes 49160 | tf_op jit(solution)/shard_map/ppermute | solution.py:563
  36.5 2.6 %collective-permute-done.1.bulk = bf16[1,2,448,2,256]{4,3,2,1,0:T(2,128)(2,1)S(1)} collective-permute-done((bf16[1,2,448,2,256]{4,3,2,1,0:T(2,128)(2,1)S(1)}, bf16[1,2,448,2,256]{4,3,2,1,0:T(2,128)(2,1)S(1)}, u32[]{:S(2)}, u32[]{:S(2)}) %collective-permute-start.1) | collective-permute-done | bytes 917536 | tf_op jit(solution)/shard_map/ppermute | solution.py:26
  39.0 2.1 %unpack.1 = (bf16[1,2,512,2,256]{4,3,2,1,0:T(2,128)(2,1)}, f32[8,128]{1,0:T(8,128)S(1)}) custom-call(s32[8,128]{1,0:T(8,128)S(1)} %get-tuple-element.27.plan, bf16[1,2,64,2,256]{4,3,2,1,0:T(2,128)(2,1)S(1)} %collective-permute-done.early, bf16[1,2,448,2,256]{4,3,2,1,0:T(2,128)(2,1)S(1)} %collective-permute-done.1.bulk), custom_call_target="tpu_custom_call" | custom-call | bytes 4194304 | tf_op jit(solution)/shard_map/unpack/pallas_call | solution.py:184
  41.2 0.5 %collective-permute-done.3.other = bf16[64,128]{1,0:T(8,128)(2,1)S(1)} collective-permute-done((bf16[64,128]{1,0:T(8,128)(2,1)S(1)}, bf16[64,128]{1,0:T(8,128)(2,1)S(1)}, u32[]{:S(2)}, u32[]{:S(2)}) %collective-permute-start.3) | collective-permute-done | bytes 16416 | tf_op jit(solution)/shard_map/ppermute | solution.py:563
  41.7 0.7 %finish.1 = (f32[1,2,64,64]{3,2,1,0:T(8,128)}, f32[1,2,64,64]{3,2,1,0:T(8,128)}) custom-call(f32[64,128]{1,0:T(8,128)S(1)} %get-tuple-element.36.kept, bf16[64,128]{1,0:T(8,128)(2,1)S(1)} %collective-permute-done.3.other, f32[2,64,64]{2,1,0:T(8,128)S(1)} %get-tuple-element.38.shown, f32[2,64,64]{2,1,0:T(8,128)S(1)} %get-tuple-element.39.step_size, ...), custom_call_target="tpu_custom_call" | custom-call | bytes 262144 | tf_op jit(solution)/shard_map/finish/pallas_call | solution.py:217
  (17 shorter events, 0.1 us)
Async XLA Ops:
  0.6 19.0 %collective-permute-start.2 = (bf16[1,2,256,2,256]{4,3,2,1,0:T(2,128)(2,1)}, bf16[1,2,256,2,256]{4,3,2,1,0:T(2,128)(2,1)S(1)}, u32[]{:S(2)}, u32[]{:S(2)}) collective-permute-start(bf16[1,2,256,2,256]{4,3,2,1,0:T(2,128)(2,1)} %param.13), channel_id=1, source_target_pairs={{256,0},{264,8},{272,16},{280,24},{288,32},{296,40},{304,48},{312,... | collective-permute-start | bytes 1572872 | tf_op jit(solution)/shard_map/ppermute | solution.py:26
  4.1 1.2 %copy-start = (bf16[1,2,512,2,256]{4,3,2,1,0:T(2,128)(2,1)S(1)}, bf16[1,2,512,2,256]{4,3,2,1,0:T(2,128)(2,1)}, u32[]{:S(2)}) copy-start(bf16[1,2,512,2,256]{4,3,2,1,0:T(2,128)(2,1)} %fresh.1) | copy-start | bytes 3145732
  5.4 0.8 %copy-start.3 = (s32[64,2,64]{2,1,0:T(2,128)S(1)}, s32[64,2,64]{2,1,0:T(2,128)}, u32[]{:S(2)}) copy-start(s32[64,2,64]{2,1,0:T(2,128)} %lists.3) | copy-start | bytes 98308
  6.2 5.7 %copy-start.1 = (bf16[1,2,512,2,256]{4,3,2,1,0:T(2,128)(2,1)S(1)}, bf16[1,2,512,2,256]{4,3,2,1,0:T(2,128)(2,1)}, u32[]{:S(2)}) copy-start(bf16[1,2,512,2,256]{4,3,2,1,0:T(2,128)(2,1)} %fresh.1) | copy-start | bytes 3145732
  8.4 11.1 %collective-permute-start = (bf16[1,2,64,2,256]{4,3,2,1,0:T(2,128)(2,1)S(1)}, bf16[1,2,64,2,256]{4,3,2,1,0:T(2,128)(2,1)S(1)}, u32[]{:S(2)}, u32[]{:S(2)}) collective-permute-start(bf16[1,2,64,2,256]{4,3,2,1,0:T(2,128)(2,1)S(1)} %get-tuple-element.28), channel_id=1, source_target_pairs={{256,0},{264,8},{272,16},{280,24},{288,32},{296,40},{304,48},{312,... | collective-permute-start | bytes 393224 | tf_op jit(solution)/shard_map/ppermute | solution.py:26
  11.9 1.2 %copy-start.10 = (bf16[1,2,512,2,256]{4,3,2,1,0:T(2,128)(2,1)S(1)}, bf16[1,2,512,2,256]{4,3,2,1,0:T(2,128)(2,1)}, u32[]{:S(2)}) copy-start(bf16[1,2,512,2,256]{4,3,2,1,0:T(2,128)(2,1)} %param.12) | copy-start | bytes 3145732
  13.1 1.0 %copy-start.2 = (bf16[1,2,512,256]{3,2,1,0:T(8,128)(2,1)S(1)}, bf16[1,2,512,256]{3,2,1,0:T(8,128)(2,1)}, u32[]{:S(2)}) copy-start(bf16[1,2,512,256]{3,2,1,0:T(8,128)(2,1)} %queries.1) | copy-start | bytes 1572868
  13.1 1.0 %copy-start.4 = (s32[64,2,64]{2,1,0:T(2,128)S(1)}, s32[64,2,64]{2,1,0:T(2,128)}, u32[]{:S(2)}) copy-start(s32[64,2,64]{2,1,0:T(2,128)} %lists.3) | copy-start | bytes 98308
  13.1 1.0 %copy-start.7 = (s32[64,2]{0,1:T(2,128)S(1)}, s32[64,2]{0,1:T(2,128)}, u32[]{:S(2)}) copy-start(s32[64,2]{0,1:T(2,128)} %param.19) | copy-start | bytes 1540
  13.3 0.9 %copy-start.6 = (s32[64,2]{0,1:T(2,128)S(1)}, s32[64,2]{0,1:T(2,128)}, u32[]{:S(2)}) copy-start(s32[64,2]{0,1:T(2,128)} %param.16) | copy-start | bytes 1540
  13.3 0.9 %copy-start.8 = (s32[64]{0:T(128)S(1)}, s32[64]{0:T(128)}, u32[]{:S(2)}) copy-start(s32[64]{0:T(128)} %requests.1) | copy-start | bytes 772
  15.1 24.0 %collective-permute-start.1 = (bf16[1,2,448,2,256]{4,3,2,1,0:T(2,128)(2,1)S(1)}, bf16[1,2,448,2,256]{4,3,2,1,0:T(2,128)(2,1)S(1)}, u32[]{:S(2)}, u32[]{:S(2)}) collective-permute-start(bf16[1,2,448,2,256]{4,3,2,1,0:T(2,128)(2,1)S(1)} %get-tuple-element.29), channel_id=1, source_target_pairs={{256,0},{264,8},{272,16},{280,24},{288,32},{296,40},{304,48},{312,... | collective-permute-start | bytes 2752520 | tf_op jit(solution)/shard_map/ppermute | solution.py:26
  19.6 0.8 %copy-start.9 = (bf16[256,64]{0,1:T(8,128)(2,1)S(1)}, bf16[256,64]{0,1:T(8,128)(2,1)}, u32[]{:S(2)}) copy-start(bf16[256,64]{0,1:T(8,128)(2,1)} %param.14) | copy-start | bytes 98308
  33.2 8.5 %copy-start.5 = (f32[1,2,64,64]{3,2,1,0:T(8,128)S(1)}, f32[1,2,64,64]{3,2,1,0:T(8,128)}, u32[]{:S(2)}) copy-start(f32[1,2,64,64]{3,2,1,0:T(8,128)} %latent.1) | copy-start | bytes 98308
  33.2 8.5 %collective-permute-start.3 = (bf16[64,128]{1,0:T(8,128)(2,1)S(1)}, bf16[64,128]{1,0:T(8,128)(2,1)S(1)}, u32[]{:S(2)}, u32[]{:S(2)}) collective-permute-start(bf16[64,128]{1,0:T(8,128)(2,1)S(1)} %get-tuple-element.37), channel_id=1, source_target_pairs={{0,1},{1,0},{2,3},{3,2},{4,5},{5,4},{6,7},{7,6},{8,9},{9,8},{10,11... | collective-permute-start | bytes 49160 | tf_op jit(solution)/shard_map/ppermute | solution.py:563
